TPU v7x, 32 devices: a whole 2x2x4 slice. The times are simulated.
32 devices in a mesh: pass: 2 (over y), az: 8 (over z, x), rg: 2 (over core).
Axes of the slice: x: 2, y: 2, z: 4, core: 2. Of those that a mesh axis runs over, the one named last changes fastest.
Arguments:
- reference_slc: bfloat16 [2, 4096, 10240], P(None, ('pass', 'az'), 'rg'), parts along dimension 1, may hold values from -8 to 8, as said below
- secondary_slc: bfloat16 [2, 4096, 10240], P(None, ('pass', 'az'), 'rg'), parts along dimension 1, may hold values from -20 to 20, as said below
- line_target: int32 [1024], P(('pass', 'az')), parts along dimension 0, may hold values from 0 to 511, as said below
- seam_partner: int32 [1024], P(('pass', 'az')), parts along dimension 0, may hold values from -1 to 63, as said below
- mask_level: int32 [1024, 512], P(('pass', 'az'), 'rg'), parts along dimension 0, may hold values from 0 to 3
Outputs:
- unwrapped: float32 [1024, 512], P(('pass', 'az'), 'rg'), parts along dimension 0
- residual: float32 [1024, 512], P(('pass', 'az'), 'rg'), parts along dimension 0
There are 2 independent parts, one for each index of `pass`. A program takes and returns all parts, laid end to end along the dimension named above; each array names one. Nothing has to cross between parts.
Inputs may be any that keep to these rules, and one draw needn't show every extreme that they name: `reference_slc`: real and imaginary planes of complex samples. `secondary_slc`: real and imaginary planes of complex samples. `line_target`: A permutation of the 512 grid rows, indexed by look row in acquisition order. Every owner of 64 grid rows receives exactly 64 look rows; no owner receives more than 16 look rows from one device, and every device sends exactly 16 look rows to at least one owner. `seam_partner`: -1 where a grid row has no partner, else the index within the next block of 64 grid rows of the row that images the same ground; the partners within a block are distinct, and the last 64 rows have none.
All inputs are finite; a program needn't handle non-finite values.
Results may differ from a plain program's by a relative error of at most 0.0003.
Values sent between devices are 32-bit elements; how exact they have to be, the bound alone decides.
A program may use at most 192 MiB of HBM per device.

v0:
```python
import math

import jax
import jax.numpy as jnp
from jax import lax
from jax.sharding import PartitionSpec as P

LOOK_AZ = 4
LOOK_RG = 20
ITERS = 2


FULL_PRECISION = lax.Precision.HIGHEST
EPSILON = 1e-06


def from_behind(value, axis, steps):
    count = lax.axis_size(axis)
    first, last = (max(0, -steps), min(count, count - steps))
    return lax.ppermute(value, axis, [(source, source + steps) for source in range(first, last)])


def with_halo(shard, sides, width):
    for axis, dim in sides:
        peers, length = (lax.axis_size(axis), shard.shape[dim])
        up = [(i, (i + 1) % peers) for i in range(peers - 1)]
        down = [(j, i) for i, j in up]
        last = lax.slice_in_dim(shard, length - width, length, axis=dim)
        first = lax.slice_in_dim(shard, 0, width, axis=dim)
        before = lax.ppermute(last, axis, up)
        after = lax.ppermute(first, axis, down)
        shard = jnp.concatenate([before, shard, after], axis=dim)
    return shard


def dct_table(freq_index, place_index, length):
    product = (2 * place_index[None, :] + 1) * freq_index[:, None] % (4 * length)
    norm_factor = jnp.where(
        freq_index == 0, math.sqrt(1.0 / length), math.sqrt(2.0 / length)
    ).astype(jnp.float32)
    return norm_factor[:, None] * jnp.cos(product.astype(jnp.float32) * (math.pi / (2.0 * length)))


def eigenvalues(freq_index, length):
    return 4.0 * jnp.sin(freq_index.astype(jnp.float32) * (math.pi / (2.0 * length))) ** 2


def neighbours(padded):
    return (
        padded[..., :-2, 1:-1],
        padded[..., 2:, 1:-1],
        padded[..., 1:-1, :-2],
        padded[..., 1:-1, 2:],
    )


def contract(left, right, left_dim, right_dim):
    return lax.dot_general(
        left,
        right,
        (((left_dim,), (right_dim,)), ((), ())),
        precision=FULL_PRECISION,
        preferred_element_type=jnp.float32,
    )


def form_looks(ref_rows, sec_rows, col_count):
    ref_real = ref_rows[0].astype(jnp.float32)
    ref_imag = ref_rows[1].astype(jnp.float32)
    sec_real = sec_rows[0].astype(jnp.float32)
    sec_imag = sec_rows[1].astype(jnp.float32)
    row_total = ref_rows.shape[1]

    def look_sum(plane):
        return plane.reshape(row_total, LOOK_AZ, col_count, LOOK_RG).sum(axis=(1, 3))

    return jnp.stack(
        [
            look_sum(ref_real * sec_real + ref_imag * sec_imag),
            look_sum(ref_imag * sec_real - ref_real * sec_imag),
            look_sum(ref_real * ref_real + ref_imag * ref_imag),
            look_sum(sec_real * sec_real + sec_imag * sec_imag),
        ]
    )


def single_product(left, right):
    return lax.psum(jnp.sum(left * right), ("az", "rg"))


def on_device(reference_slc, secondary_slc, line_target, seam_partner, mask_level):
    dev_count = lax.axis_size("az")
    rg_count = lax.axis_size("rg")
    az_place = lax.axis_index("az")
    rg_place = lax.axis_index("rg")
    row_count = line_target.shape[0]
    col_count = mask_level.shape[1]
    sample_count = reference_slc.shape[2]
    capacity = max(2, 2 * row_count // dev_count)
    reference_rows = reference_slc.reshape(2, row_count, LOOK_AZ, sample_count)
    secondary_rows = secondary_slc.reshape(2, row_count, LOOK_AZ, sample_count)
    owners = line_target // row_count
    local_index = jnp.arange(row_count, dtype=jnp.int32)
    earlier = (owners[:, None] == owners[None, :]) & (local_index[None, :] < local_index[:, None])
    slot_rank = jnp.sum(earlier.astype(jnp.int32), axis=1)
    slot_index = owners * capacity + slot_rank
    buffer_length = dev_count * capacity
    source_row = jnp.full((buffer_length,), row_count, jnp.int32).at[slot_index].set(local_index)
    positions = (
        jnp.full((1, buffer_length), row_count, jnp.int32)
        .at[0, slot_index]
        .set(line_target % row_count)
    )
    local_sums = form_looks(reference_rows, secondary_rows, col_count)
    sent_sums = jnp.take(local_sums, source_row, axis=1, mode="fill", fill_value=0.0)
    got_sums, got_positions = (
        lax.all_to_all(sent_sums, "az", split_axis=1, concat_axis=1, tiled=True),
        lax.all_to_all(positions, "az", split_axis=1, concat_axis=1, tiled=True),
    )
    gridded = jnp.zeros_like(local_sums).at[:, got_positions[0]].set(got_sums, mode="drop")
    next_block = from_behind(gridded, "az", -1)
    has_partner = seam_partner >= 0
    picked = jnp.take(next_block, jnp.maximum(seam_partner, 0), axis=1)
    combined = gridded + jnp.where(has_partner[None, :, None], picked, 0.0)
    magnitude = jnp.sqrt(combined[2] * combined[3]) + EPSILON
    weight = (1 + mask_level).astype(jnp.float32) * 0.25
    fields = jnp.stack([combined[0] / magnitude, combined[1] / magnitude, weight])
    padded = with_halo(fields, (("az", 1), ("rg", 2)), 1)
    beside_all = neighbours(padded)
    edge_weights = [weight * item[2] for item in beside_all]
    right_side = jnp.zeros((row_count, col_count), jnp.float32)
    for edge, item in zip(edge_weights, beside_all):
        right_side = right_side + edge * (fields[1] * item[0] - fields[0] * item[1])
    damping = 0.25 / (row_count * row_count)
    grid_rows = row_count * dev_count
    grid_cols = col_count * rg_count
    my_cols = rg_place * col_count + jnp.arange(col_count, dtype=jnp.int32)
    column_width = col_count // dev_count
    all_rows = jnp.arange(grid_rows, dtype=jnp.int32)
    full_basis = dct_table(all_rows, all_rows, grid_rows)
    pencil_cols = (
        rg_place * col_count + az_place * column_width + jnp.arange(column_width, dtype=jnp.int32)
    )
    pencil_divisor = (
        eigenvalues(pencil_cols, grid_cols)[:, None]
        + eigenvalues(all_rows, grid_rows)[None, :]
        + damping
    )

    def precondition(values):
        basis_block = dct_table(
            jnp.arange(col_count * lax.axis_size("rg"), dtype=jnp.int32), my_cols, grid_cols
        )
        range_spectrum = lax.psum_scatter(
            contract(basis_block, values, 1, 1), "rg", scatter_dimension=0, tiled=True
        )
        pencil = lax.all_to_all(range_spectrum, "az", split_axis=0, concat_axis=1, tiled=True)
        filtered = contract(pencil, full_basis, 1, 1) / pencil_divisor
        restored = contract(filtered, full_basis, 1, 0)
        back_columns = lax.all_to_all(restored, "az", split_axis=1, concat_axis=0, tiled=True)
        basis_block = dct_table(
            my_cols, jnp.arange(col_count * lax.axis_size("rg"), dtype=jnp.int32), grid_cols
        )
        return lax.psum_scatter(
            contract(basis_block, back_columns, 0, 0), "rg", scatter_dimension=0, tiled=True
        ).T

    solution = jnp.zeros((row_count, col_count), jnp.float32)
    residual = right_side
    precond = precondition(residual)
    direction = precond
    inner_now = single_product(residual, precond)
    for turn_index in range(ITERS):
        rim = with_halo(direction, (("az", 0), ("rg", 1)), 1)
        result_sum = damping * direction
        for apply_edge, apply_item in zip(edge_weights, neighbours(rim)):
            result_sum = result_sum + apply_edge * (direction - apply_item)
        step_size = inner_now / lax.psum(jnp.sum(direction * result_sum), ("az", "rg"))
        solution = solution + step_size * direction
        residual = residual - step_size * result_sum
        if turn_index + 1 < ITERS:
            precond = precondition(residual)
            inner_next = single_product(residual, precond)
            direction = precond + inner_next / inner_now * direction
            inner_now = inner_next
    return (solution, residual)


def solution(mesh):
    in_specs = (
        P(None, ("pass", "az"), "rg"),
        P(None, ("pass", "az"), "rg"),
        P(("pass", "az")),
        P(("pass", "az")),
        P(("pass", "az"), "rg"),
    )
    out_specs = (P(("pass", "az"), "rg"), P(("pass", "az"), "rg"))
    return jax.shard_map(
        on_device, mesh=mesh, in_specs=in_specs, out_specs=out_specs, check_vma=False
    )
```

profile of v0, /device:TPU:0, one launch (start us, length us, event | category | flops | bytes accessed | tf_op | source)
XLA Modules:
  0.0 548.7 jit_solution(4348910988675888694)
XLA Ops:
  9.5 7.3 %all-to-all-start = ((s32[1,8,16]{2,0,1:T(1,128)}), s32[1,8,16]{2,0,1:T(1,128)S(1)}, u32[]{:S(2)}, u32[]{:S(2)}) async-start(s32[1,8,16]{2,0,1:T(1,128)} %bitcast), calls=%async_computation | async-start | bytes 8192 | tf_op jit(solution)/shard_map/all_to_all | solution.py:118
  17.6 11.4 %fusion.1 = (f32[1,256,5120]{2,1,0:T(8,128)}, f32[1,256,5120]{2,1,0:T(8,128)}, f32[1,256,5120]{2,1,0:T(8,128)}, f32[1,256,5120]{2,1,0:T(8,128)}) fusion(bf16[2,256,5120]{2,1,0:T(8,128)(2,1)} %param.6, bf16[2,256,5120]{2,1,0:T(8,128)(2,1)} %param.5), kind=kLoop, calls=%fused_computation.14 | loop fusion | flops 20971520 | bytes 31457280 | tf_op jit(solution)/shard_map/add | solution.py:79
  29.0 41.4 %add.254 = f32[64,4,256,20]{3,2,1,0:T(8,128)} reshape(f32[1,256,5120]{2,1,0:T(8,128)} %get-tuple-element.14) | data formatting | bytes 10485760 | tf_op jit(solution)/shard_map/add | solution.py:79
  70.4 12.2 %reduce_sum.82 = f32[64,256]{1,0:T(8,128)S(1)} reduce(f32[64,4,256,20]{3,2,1,0:T(8,128)} %add.254, f32[]{:T(128)} %constant.79.clone.1), dimensions={1,3}, to_apply=%region_3.4 | reduce | flops 1294336 | bytes 5308420 | tf_op jit(solution)/shard_map/reduce_sum | solution.py:75
  82.6 41.4 %sub.61 = f32[64,4,256,20]{3,2,1,0:T(8,128)} reshape(f32[1,256,5120]{2,1,0:T(8,128)} %get-tuple-element.15) | data formatting | bytes 10485760 | tf_op jit(solution)/shard_map/sub | solution.py:80
  124.0 12.2 %reduce_sum.83 = f32[64,256]{1,0:T(8,128)S(1)} reduce(f32[64,4,256,20]{3,2,1,0:T(8,128)} %sub.61, f32[]{:T(128)} %constant.79.clone.1), dimensions={1,3}, to_apply=%region_4.5 | reduce | flops 1294336 | bytes 5308420 | tf_op jit(solution)/shard_map/reduce_sum | solution.py:75
  136.3 41.4 %add.256 = f32[64,4,256,20]{3,2,1,0:T(8,128)} reshape(f32[1,256,5120]{2,1,0:T(8,128)} %get-tuple-element.16) | data formatting | bytes 10485760 | tf_op jit(solution)/shard_map/add | solution.py:81
  177.7 12.2 %reduce_sum.84 = f32[64,256]{1,0:T(8,128)S(1)} reduce(f32[64,4,256,20]{3,2,1,0:T(8,128)} %add.256, f32[]{:T(128)} %constant.79.clone.1), dimensions={1,3}, to_apply=%region_5.6 | reduce | flops 1294336 | bytes 5308420 | tf_op jit(solution)/shard_map/reduce_sum | solution.py:75
  189.9 41.4 %add.258 = f32[64,4,256,20]{3,2,1,0:T(8,128)} reshape(f32[1,256,5120]{2,1,0:T(8,128)} %get-tuple-element.17) | data formatting | bytes 10485760 | tf_op jit(solution)/shard_map/add | solution.py:82
  231.3 12.2 %reduce_sum.85 = f32[64,256]{1,0:T(8,128)S(1)} reduce(f32[64,4,256,20]{3,2,1,0:T(8,128)} %add.258, f32[]{:T(128)} %constant.79.clone.1), dimensions={1,3}, to_apply=%region_6.7 | reduce | flops 1294336 | bytes 5308420 | tf_op jit(solution)/shard_map/reduce_sum | solution.py:75
  245.8 6.0 %all-to-all-start.1 = ((f32[4,128,256]{2,0,1:T(4,128)}), f32[4,128,256]{2,0,1:T(4,128)S(1)}, u32[]{:S(2)}, u32[]{:S(2)}) async-start(f32[4,128,256]{2,0,1:T(4,128)} %select_bitcast_fusion), calls=%async_computation.1 | async-start | bytes 1048576 | tf_op jit(solution)/shard_map/all_to_all | solution.py:117
  253.1 12.6 %all-to-all-done.1 = f32[4,128,256]{2,0,1:T(4,128)S(1)} async-done(((f32[4,128,256]{2,0,1:T(4,128)}), f32[4,128,256]{2,0,1:T(4,128)S(1)}, u32[]{:S(2)}, u32[]{:S(2)}) %all-to-all-start.1) | async-done | bytes 524320 | tf_op jit(solution)/shard_map/all_to_all | solution.py:117
  271.6 7.3 %collective-permute-done = f32[4,64,256]{2,0,1:T(4,128)S(1)} collective-permute-done((f32[4,64,256]{2,0,1:T(4,128)S(1)}, f32[4,64,256]{2,0,1:T(4,128)S(1)}, u32[]{:S(2)}, u32[]{:S(2)}) %collective-permute-start) | collective-permute-done | bytes 262176 | tf_op jit(solution)/shard_map/ppermute | solution.py:20
  298.1 5.8 %reduce-scatter.5.cloned.1.call-done = f32[256,64]{0,1:T(8,128)} async-done(((f32[512,64]{0,1:T(8,128)}), f32[256,64]{0,1:T(8,128)}) %reduce-scatter.5.cloned.1.call-update) | async-done | bytes 65552 | tf_op jit(solution)/shard_map/reduce_scatter | solution.py:154
  305.6 5.7 %all-to-all-start.2 = ((f32[8,1,2048]{2,1,0:T(1,128)}), f32[8,1,2048]{2,1,0:T(1,128)S(1)}, u32[]{:S(2)}, u32[]{:S(2)}) async-start(f32[8,1,2048]{2,1,0:T(1,128)} %reshape.228), calls=%async_computation.3 | async-start | bytes 131072 | tf_op jit(solution)/shard_map/all_to_all | solution.py:157
  311.4 6.8 %all-to-all-done.2 = f32[8,1,2048]{2,1,0:T(1,128)S(1)} async-done(((f32[8,1,2048]{2,1,0:T(1,128)}), f32[8,1,2048]{2,1,0:T(1,128)S(1)}, u32[]{:S(2)}, u32[]{:S(2)}) %all-to-all-start.2) | async-done | bytes 65568 | tf_op jit(solution)/shard_map/all_to_all | solution.py:157
  333.6 10.6 %reduce-scatter.7.cloned.1.call-start = ((), (), s32[]{:S(2)}) async-start(), calls=%async_computation.11 | async-start | bytes 196608 | tf_op jit(solution)/shard_map/reduce_scatter | solution.py:164
  348.2 8.8 %reduce-scatter.7.cloned.1.call-done = f32[256,64]{0,1:T(8,128)} async-done(((f32[512,64]{0,1:T(8,128)}), f32[256,64]{0,1:T(8,128)}) %reduce-scatter.7.cloned.1.call-update) | async-done | bytes 65552 | tf_op jit(solution)/shard_map/reduce_scatter | solution.py:164
  374.1 32.4 %all-reduce.1 = (f32[]{:T(128)}, f32[]{:T(128)}) all-reduce(f32[]{:T(128)} %get-tuple-element.3, f32[]{:T(128)} %get-tuple-element.2), channel_id=1, replica_groups=mesh['pass'=2,'az'=8,'rg'=2] {'az','rg'}, use_global_device_ids=true, to_apply=%region_11.12 | all-reduce | flops 2 | bytes 16 | tf_op jit(solution)/shard_map/psum | solution.py:88
  417.3 12.4 %all_to_all.90 = f32[8,1,2048]{2,1,0:T(1,128)S(1)} all-to-all(f32[8,1,2048]{2,1,0:T(1,128)S(1)} %reshape.232), channel_id=1, replica_groups=mesh['pass'=2,'az'=8,'rg'=2] {'az'}, dimensions={0} | all-to-all | bytes 131072 | tf_op jit(solution)/shard_map/all_to_all | solution.py:157
  440.5 9.5 %all_to_all.91 = f32[8,1,2048]{2,1,0:T(1,128)S(1)} all-to-all(f32[8,1,2048]{2,1,0:T(1,128)S(1)} %reshape.234), channel_id=1, replica_groups=mesh['pass'=2,'az'=8,'rg'=2] {'az'}, dimensions={0} | all-to-all | bytes 131072 | tf_op jit(solution)/shard_map/all_to_all | solution.py:160
  454.0 5.2 reduce-scatter.11.cloned.1.call-done
  460.7 34.5 %psum.30 = f32[]{:T(128)} all-reduce(f32[]{:T(128)} %fusion.89), channel_id=1, replica_groups=mesh['pass'=2,'az'=8,'rg'=2] {'az','rg'}, use_global_device_ids=true, to_apply=%region_17.18 | all-reduce | flops 1 | bytes 8 | tf_op jit(solution)/shard_map/psum | solution.py:88
  509.7 30.3 %psum.31 = f32[]{:T(128)} all-reduce(f32[]{:T(128)} %get-tuple-element.6), channel_id=1, replica_groups=mesh['pass'=2,'az'=8,'rg'=2] {'az','rg'}, use_global_device_ids=true, to_apply=%region_19.20 | all-reduce | flops 1 | bytes 8 | tf_op jit(solution)/shard_map/psum | solution.py:178
  (126 shorter events, 109.2 us)
Async XLA Ops:
  9.5 236.3 %all-to-all-start = ((s32[1,8,16]{2,0,1:T(1,128)}), s32[1,8,16]{2,0,1:T(1,128)S(1)}, u32[]{:S(2)}, u32[]{:S(2)}) async-start(s32[1,8,16]{2,0,1:T(1,128)} %bitcast), calls=%async_computation | async-start | bytes 8192 | tf_op jit(solution)/shard_map/all_to_all | solution.py:118
  231.3 20.5 %copy-start.2 = (s32[64]{0:T(128)S(1)}, s32[64]{0:T(128)}, u32[]{:S(2)}) copy-start(s32[64]{0:T(128)} %param.8) | copy-start | bytes 772
  243.5 28.0 %copy-start.1 = (s32[64,256]{1,0:T(8,128)S(1)}, s32[64,256]{1,0:T(8,128)}, u32[]{:S(2)}) copy-start(s32[64,256]{1,0:T(8,128)} %param.9) | copy-start | bytes 196612
  245.8 20.0 %all-to-all-start.1 = ((f32[4,128,256]{2,0,1:T(4,128)}), f32[4,128,256]{2,0,1:T(4,128)S(1)}, u32[]{:S(2)}, u32[]{:S(2)}) async-start(f32[4,128,256]{2,0,1:T(4,128)} %select_bitcast_fusion), calls=%async_computation.1 | async-start | bytes 1048576 | tf_op jit(solution)/shard_map/all_to_all | solution.py:117
  251.8 52.2 %reduce-scatter.5.cloned.1.call-start = ((), (), s32[]{:S(2)}) async-start(), calls=%async_computation.10 | async-start | bytes 196608 | tf_op jit(solution)/shard_map/reduce_scatter | solution.py:154
  270.3 8.6 %collective-permute-start = (f32[4,64,256]{2,0,1:T(4,128)S(1)}, f32[4,64,256]{2,0,1:T(4,128)S(1)}, u32[]{:S(2)}, u32[]{:S(2)}) collective-permute-start(f32[4,64,256]{2,0,1:T(4,128)S(1)} %scatter_fusion), channel_id=1, source_target_pairs={{2,0},{4,2},{6,4},{8,6},{10,8},{12,10},{14,12},{3,1},{5,3},{7,5},{... | collective-permute-start | bytes 786440 | tf_op jit(solution)/shard_map/ppermute | solution.py:20
  279.9 5.9 %collective-permute-start.1 = (f32[3,1,256]{2,1,0:T(1,128)S(1)}, f32[3,1,256]{2,1,0:T(1,128)S(1)}, u32[]{:S(2)}, u32[]{:S(2)}) collective-permute-start(f32[3,1,256]{2,1,0:T(1,128)S(1)} %get-tuple-element.22), channel_id=1, source_target_pairs={{0,2},{2,4},{4,6},{6,8},{8,10},{10,12},{12,14},{1,3},{3,5},{5,7},{... | collective-permute-start | bytes 9224 | tf_op jit(solution)/shard_map/ppermute | solution.py:30
  284.4 5.5 %collective-permute-start.2 = (f32[3,1,256]{2,1,0:T(1,128)S(1)}, f32[3,1,256]{2,1,0:T(1,128)S(1)}, u32[]{:S(2)}, u32[]{:S(2)}) collective-permute-start(f32[3,1,256]{2,1,0:T(1,128)S(1)} %get-tuple-element.23), channel_id=1, source_target_pairs={{2,0},{4,2},{6,4},{8,6},{10,8},{12,10},{14,12},{3,1},{5,3},{7,5},{... | collective-permute-start | bytes 9224 | tf_op jit(solution)/shard_map/ppermute | solution.py:31
  290.0 2.9 collective-permute-start.3
  291.3 3.2 collective-permute-start.4
  305.6 12.6 %all-to-all-start.2 = ((f32[8,1,2048]{2,1,0:T(1,128)}), f32[8,1,2048]{2,1,0:T(1,128)S(1)}, u32[]{:S(2)}, u32[]{:S(2)}) async-start(f32[8,1,2048]{2,1,0:T(1,128)} %reshape.228), calls=%async_computation.3 | async-start | bytes 131072 | tf_op jit(solution)/shard_map/all_to_all | solution.py:157
  330.2 14.0 %all-to-all-start.3 = ((f32[8,1,2048]{2,1,0:T(1,128)}), f32[8,1,2048]{2,1,0:T(1,128)S(1)}, u32[]{:S(2)}, u32[]{:S(2)}) async-start(f32[8,1,2048]{2,1,0:T(1,128)} %reshape.230), calls=%async_computation.4 | async-start | bytes 131072 | tf_op jit(solution)/shard_map/all_to_all | solution.py:160
  333.6 23.4 %reduce-scatter.7.cloned.1.call-start = ((), (), s32[]{:S(2)}) async-start(), calls=%async_computation.11 | async-start | bytes 196608 | tf_op jit(solution)/shard_map/reduce_scatter | solution.py:164
  348.2 68.0 %reduce-scatter.9.cloned.1.call-start = ((), (), s32[]{:S(2)}) async-start(), calls=%async_computation.12 | async-start | bytes 196608 | tf_op jit(solution)/shard_map/reduce_scatter | solution.py:154
  357.7 4.9 collective-permute-start.5
  361.3 5.5 collective-permute-start.6
  367.7 2.6 collective-permute-start.7
  369.0 3.1 collective-permute-start.8
  411.2 48.0 %reduce-scatter.11.cloned.1.call-start = ((), (), s32[]{:S(2)}) async-start(), calls=%async_computation.13 | async-start | bytes 196608 | tf_op jit(solution)/shard_map/reduce_scatter | solution.py:164
  435.7 60.8 %copy-start = (f32[256,64]{0,1:T(8,128)S(1)}, f32[256,64]{0,1:T(8,128)}, u32[]{:S(2)}) copy-start(f32[256,64]{0,1:T(8,128)} %reduce-scatter.7.cloned.1.call-done) | copy-start | bytes 196612
  497.3 5.9 %collective-permute-start.10 = (f32[1,256]{1,0:T(1,128)S(1)}, f32[1,256]{1,0:T(1,128)S(1)}, u32[]{:S(2)}, u32[]{:S(2)}) collective-permute-start(f32[1,256]{1,0:T(1,128)S(1)} %get-tuple-element.29), channel_id=1, source_target_pairs={{2,0},{4,2},{6,4},{8,6},{10,8},{12,10},{14,12},{3,1},{5,3},{7,5},{... | collective-permute-start | bytes 3080 | tf_op jit(solution)/shard_map/ppermute | solution.py:31
  498.6 5.8 %collective-permute-start.9 = (f32[1,256]{1,0:T(1,128)S(1)}, f32[1,256]{1,0:T(1,128)S(1)}, u32[]{:S(2)}, u32[]{:S(2)}) collective-permute-start(f32[1,256]{1,0:T(1,128)S(1)} %get-tuple-element.28), channel_id=1, source_target_pairs={{0,2},{2,4},{4,6},{6,8},{8,10},{10,12},{12,14},{1,3},{3,5},{5,7},{... | collective-permute-start | bytes 3080 | tf_op jit(solution)/shard_map/ppermute | solution.py:30
  504.6 2.6 collective-permute-start.11
  505.9 3.1 collective-permute-start.12
Sparse Core Ops, SparseCore 0:
  298.2 5.6 reduce-scatter.4
  348.3 8.6 reduce-scatter.6
  411.4 4.8 reduce-scatter.8
  454.1 5.0 reduce-scatter.10
where the time goes:
time: 555 us; the launch traced here: 549 us
  local copies, waits for them, and re-layouts  181 us (33%)
  blocking collectives  119 us (21%)
  other arithmetic  73.5 us (13%)
  waiting for transfers between devices  66.3 us (12%)
  starting transfers between devices  58.9 us (11%)
  matrix products  31.7 us (6%)
  between operations  18.6 us (3%)
    psum x2, blocking collectives, single_product(): return lax.psum(jnp.sum(left * right), ('az', 'rg'))  66.9 us
    reduce_sum x4, other arithmetic, look_sum(): plane.reshape(row_total, LOOK_AZ, col_count, LOOK_RG).sum(axis=(1, 3))  48.8 us
    add x1, local copies, waits for them, and re-layouts, form_looks(): sec_real * sec_real + sec_imag * sec_imag  41.4 us
    sub x1, local copies, waits for them, and re-layouts, form_looks(): ref_imag * sec_real - ref_real * sec_imag  41.4 us
    add x1, local copies, waits for them, and re-layouts, form_looks(): ref_real * ref_real + ref_imag * ref_imag  41.4 us
    add x1, local copies, waits for them, and re-layouts, form_looks(): ref_real * sec_real + ref_imag * sec_imag  41.4 us
    dot_general x8, matrix products, contract(): lax.dot_general(left, right, (((left_dim,), (right_dim,)), ((), ())), pre...  31.7 us
    psum x1, blocking collectives, on_device(): lax.psum(jnp.sum(direction * result_sum), ('az', 'rg'))  30.3 us
  transfers between devices with their start and end apart: 21, of which 13 were waited for; matrix products, arithmetic and copies ran while one was open for 42% of the time, Pallas kernels for 0%

commit v1 on v0

--- a/solution.py
+++ b/solution.py
@@ -1,8 +1,12 @@
+import functools
 import math
 
 import jax
 import jax.numpy as jnp
+import numpy as np
 from jax import lax
+from jax.experimental import pallas as pl
+from jax.experimental.pallas import tpu as pltpu
 from jax.sharding import PartitionSpec as P
 
 LOOK_AZ = 4
@@ -64,24 +68,62 @@
     )
 
 
-def form_looks(ref_rows, sec_rows, col_count):
-    ref_real = ref_rows[0].astype(jnp.float32)
-    ref_imag = ref_rows[1].astype(jnp.float32)
-    sec_real = sec_rows[0].astype(jnp.float32)
-    sec_imag = sec_rows[1].astype(jnp.float32)
-    row_total = ref_rows.shape[1]
-
-    def look_sum(plane):
-        return plane.reshape(row_total, LOOK_AZ, col_count, LOOK_RG).sum(axis=(1, 3))
-
-    return jnp.stack(
-        [
-            look_sum(ref_real * sec_real + ref_imag * sec_imag),
-            look_sum(ref_imag * sec_real - ref_real * sec_imag),
-            look_sum(ref_real * ref_real + ref_imag * ref_imag),
-            look_sum(sec_real * sec_real + sec_imag * sec_imag),
-        ]
-    )
+CHUNK = 256
+
+
+def look_kernel(lines, half, ref_ref, sec_ref, group_ref, line_ref, out_ref):
+    step_rows = lines // LOOK_AZ
+    width = half // LOOK_RG
+    for side in range(out_ref.shape[2] // width):
+        total = jnp.zeros((8 * lines, width), jnp.float32)
+        for start in range(0, half, CHUNK):
+            span = pl.ds(side * half + start, CHUNK)
+            mr = ref_ref[0, :, span].astype(jnp.float32)
+            mi = ref_ref[1, :, span].astype(jnp.float32)
+            sr = sec_ref[0, :, span].astype(jnp.float32)
+            si = sec_ref[1, :, span].astype(jnp.float32)
+            planes = jnp.concatenate(
+                [mr * sr + mi * si, mi * sr - mr * si, mr * mr + mi * mi, sr * sr + si * si], axis=0
+            )
+            high = planes.astype(jnp.bfloat16)
+            low = (planes - high.astype(jnp.float32)).astype(jnp.bfloat16)
+            total = total + jnp.dot(
+                jnp.concatenate([high, low], axis=0),
+                group_ref[pl.ds(start, CHUNK), :],
+                preferred_element_type=jnp.float32,
+            )
+        joined = total[: 4 * lines] + total[4 * lines :]
+        sums = jnp.dot(
+            line_ref[...], joined, precision=FULL_PRECISION, preferred_element_type=jnp.float32
+        )
+        for plane in range(4):
+            out_ref[plane, :, side * width : (side + 1) * width] = sums[
+                plane * step_rows : (plane + 1) * step_rows
+            ]
+
+
+def form_looks(ref_lines, sec_lines, col_count):
+    line_count, sample_count = ref_lines.shape[1:]
+    lines = 32
+    half = 128 * LOOK_RG
+    group = (np.arange(half)[:, None] // LOOK_RG == np.arange(128)[None, :]).astype(jnp.bfloat16)
+    line_of = (np.arange(4 * lines)[None, :] // LOOK_AZ == np.arange(lines)[:, None]).astype(
+        np.float32
+    )
+    block = pl.BlockSpec((2, lines, sample_count), lambda i: (0, i, 0))
+    return pl.pallas_call(
+        functools.partial(look_kernel, lines, half),
+        grid=(line_count // lines,),
+        in_specs=[
+            block,
+            block,
+            pl.BlockSpec(group.shape, lambda i: (0, 0)),
+            pl.BlockSpec(line_of.shape, lambda i: (0, 0)),
+        ],
+        out_specs=pl.BlockSpec((4, lines // LOOK_AZ, col_count), lambda i: (0, i, 0)),
+        out_shape=jax.ShapeDtypeStruct((4, line_count // LOOK_AZ, col_count), jnp.float32),
+        name="form_looks",
+    )(ref_lines, sec_lines, group, line_of)
 
 
 def single_product(left, right):
@@ -95,10 +137,7 @@
     rg_place = lax.axis_index("rg")
     row_count = line_target.shape[0]
     col_count = mask_level.shape[1]
-    sample_count = reference_slc.shape[2]
     capacity = max(2, 2 * row_count // dev_count)
-    reference_rows = reference_slc.reshape(2, row_count, LOOK_AZ, sample_count)
-    secondary_rows = secondary_slc.reshape(2, row_count, LOOK_AZ, sample_count)
     owners = line_target // row_count
     local_index = jnp.arange(row_count, dtype=jnp.int32)
     earlier = (owners[:, None] == owners[None, :]) & (local_index[None, :] < local_index[:, None])
@@ -111,7 +150,7 @@
         .at[0, slot_index]
         .set(line_target % row_count)
     )
-    local_sums = form_looks(reference_rows, secondary_rows, col_count)
+    local_sums = form_looks(reference_slc, secondary_slc, col_count)
     sent_sums = jnp.take(local_sums, source_row, axis=1, mode="fill", fill_value=0.0)
     got_sums, got_positions = (
         lax.all_to_all(sent_sums, "az", split_axis=1, concat_axis=1, tiled=True),

time: 555 us -> 330 us (0.59)
  local copies, waits for them, and re-layouts: 181 us -> 16.1 us
  other arithmetic: 73.5 us -> 13 us
  Pallas kernels: 0 us -> 12.4 us
  starting transfers between devices: 58.9 us -> 48.3 us
    add x3 -> x0, local copies, waits for them, and re-layouts: 124 us -> none  [the longest x1 41.4 us: form_looks(): sec_real * sec_real + sec_imag * sec_imag]
    reduce_sum x4 -> x0, other arithmetic: 48.8 us -> none  [look_sum(): plane.reshape(row_total, LOOK_AZ, col_count, LOOK_RG).sum(axis=(1, 3))]
    sub x1 -> x0, local copies, waits for them, and re-layouts: 41.4 us -> none  [form_looks(): ref_imag * sec_real - ref_real * sec_imag]
    pallas_call x0 -> x1, Pallas kernels: none -> 12.4 us  [form_looks(): pl.pallas_call(functools.partial(look_kernel, lines, half), grid=(line_co...]
    add x1 -> x0, other arithmetic: 11.4 us -> none  [form_looks(): ref_real * sec_real + ref_imag * sec_imag]
    reduce_scatter x2, starting transfers between devices: 10.6 us -> 0.3 us  [precondition(): lax.psum_scatter(contract(basis_block, back_columns, 0, 0), 'rg', scatter...]
    all_to_all x1, waiting for transfers between devices: 0.01 us -> 6.55 us  [precondition(): lax.all_to_all(restored, 'az', split_axis=1, concat_axis=0, tiled=True)]
  transfers between devices with their start and end apart: 21 -> 21, of which waited for: 13 -> 14; matrix products, arithmetic and copies ran while one was open for 42% -> 2% of each run, Pallas kernels for 0% -> 4%
where the time goes in v1:
time: 330 us; the launch traced here: 328 us
  blocking collectives  119 us (36%)
  waiting for transfers between devices  69.6 us (21%)
  starting transfers between devices  48.3 us (15%)
  matrix products  31.7 us (10%)
  between operations  18.3 us (6%)
  local copies, waits for them, and re-layouts  16.1 us (5%)
  other arithmetic  13 us (4%)
  Pallas kernels  12.4 us (4%)
    psum x2, blocking collectives, single_product(): return lax.psum(jnp.sum(left * right), ('az', 'rg'))  67 us
    dot_general x8, matrix products, contract(): lax.dot_general(left, right, (((left_dim,), (right_dim,)), ((), ())), pre...  31.7 us
    psum x1, blocking collectives, on_device(): lax.psum(jnp.sum(direction * result_sum), ('az', 'rg'))  30.3 us
    ppermute x6, starting transfers between devices, with_halo(): before = lax.ppermute(last, axis, up)  16.5 us
    ppermute x6, waiting for transfers between devices, with_halo(): after = lax.ppermute(first, axis, down)  13.8 us
    all_to_all x1, waiting for transfers between devices, on_device(): lax.all_to_all(sent_sums, 'az', split_axis=1, concat_axis=1, tiled=True)  12.6 us
    pallas_call x1, Pallas kernels, form_looks(): pl.pallas_call(functools.partial(look_kernel, lines, half), grid=(line_co...  12.4 us
    all_to_all x1, blocking collectives, precondition(): lax.all_to_all(range_spectrum, 'az', split_axis=0, concat_axis=1, tiled=T...  12.4 us
  transfers between devices with their start and end apart: 21, of which 14 were waited for; matrix products, arithmetic and copies ran while one was open for 2% of the time, Pallas kernels for 4%

profile of v1, /device:TPU:0, one launch (start us, length us, event | category | flops | bytes accessed | tf_op | source)
XLA Modules:
  0.0 328.2 jit_solution(1951042164170768182)
XLA Ops:
  9.5 7.3 %all-to-all-start = ((s32[1,8,16]{2,0,1:T(1,128)}), s32[1,8,16]{2,0,1:T(1,128)S(1)}, u32[]{:S(2)}, u32[]{:S(2)}) async-start(s32[1,8,16]{2,0,1:T(1,128)} %bitcast), calls=%async_computation | async-start | bytes 8192 | tf_op jit(solution)/shard_map/all_to_all | solution.py:157
  17.6 12.4 %form_looks.1 = f32[4,64,256]{2,1,0:T(8,128)} custom-call(bf16[2,256,5120]{2,1,0:T(8,128)(2,1)} %ref_ref.1, bf16[2,256,5120]{2,1,0:T(8,128)(2,1)} %sec_ref.1, bf16[2560,128]{1,0:T(8,128)(2,1)} %constant.148.clone.group_ref, f32[32,128]{1,0:T(8,128)} %constant.149.clone.line_ref), custom_call_target="tpu_custom_call" | custom-call | tf_op jit(solution)/shard_map/form_looks/pallas_call | solution.py:114
  33.1 6.0 %all-to-all-start.1 = ((f32[4,128,256]{2,0,1:T(4,128)}), f32[4,128,256]{2,0,1:T(4,128)S(1)}, u32[]{:S(2)}, u32[]{:S(2)}) async-start(f32[4,128,256]{2,0,1:T(4,128)} %select_bitcast_fusion), calls=%async_computation.1 | async-start | bytes 1048576 | tf_op jit(solution)/shard_map/all_to_all | solution.py:156
  40.4 12.6 %all-to-all-done.1 = f32[4,128,256]{2,0,1:T(4,128)S(1)} async-done(((f32[4,128,256]{2,0,1:T(4,128)}), f32[4,128,256]{2,0,1:T(4,128)S(1)}, u32[]{:S(2)}, u32[]{:S(2)}) %all-to-all-start.1) | async-done | bytes 524320 | tf_op jit(solution)/shard_map/all_to_all | solution.py:156
  53.1 4.5 %scatter_fusion = f32[4,64,256]{2,0,1:T(4,128)S(1)} fusion(f32[4,64,256]{2,0,1:T(4,128)S(1)} %broadcast_in_dim.90, s32[128]{0:T(128)S(1)} %fusion.89, f32[128,4,256]{2,1,0:T(4,128)S(1)} %bitcast.95), kind=kCustom, calls=%fused_computation.4 | custom fusion | bytes 1573376 | tf_op jit(solution)/shard_map/scatter | solution.py:159
  58.9 7.3 %collective-permute-done = f32[4,64,256]{2,0,1:T(4,128)S(1)} collective-permute-done((f32[4,64,256]{2,0,1:T(4,128)S(1)}, f32[4,64,256]{2,0,1:T(4,128)S(1)}, u32[]{:S(2)}, u32[]{:S(2)}) %collective-permute-start) | collective-permute-done | bytes 262176 | tf_op jit(solution)/shard_map/ppermute | solution.py:24
  67.2 4.5 %collective-permute-start.1 = (f32[3,1,256]{2,1,0:T(1,128)S(1)}, f32[3,1,256]{2,1,0:T(1,128)S(1)}, u32[]{:S(2)}, u32[]{:S(2)}) collective-permute-start(f32[3,1,256]{2,1,0:T(1,128)S(1)} %get-tuple-element.18), channel_id=1, source_target_pairs={{0,2},{2,4},{4,6},{6,8},{8,10},{10,12},{12,14},{1,3},{3,5},{5,7},{... | collective-permute-start | bytes 9224 | tf_op jit(solution)/shard_map/ppermute | solution.py:34
  85.4 5.8 %reduce-scatter.5.cloned.1.call-done = f32[256,64]{0,1:T(8,128)} async-done(((f32[512,64]{0,1:T(8,128)}), f32[256,64]{0,1:T(8,128)}) %reduce-scatter.5.cloned.1.call-update) | async-done | bytes 65552 | tf_op jit(solution)/shard_map/reduce_scatter | solution.py:193
  92.9 5.7 %all-to-all-start.2 = ((f32[8,1,2048]{2,1,0:T(1,128)}), f32[8,1,2048]{2,1,0:T(1,128)S(1)}, u32[]{:S(2)}, u32[]{:S(2)}) async-start(f32[8,1,2048]{2,1,0:T(1,128)} %reshape.186), calls=%async_computation.3 | async-start | bytes 131072 | tf_op jit(solution)/shard_map/all_to_all | solution.py:196
  98.7 6.8 %all-to-all-done.2 = f32[8,1,2048]{2,1,0:T(1,128)S(1)} async-done(((f32[8,1,2048]{2,1,0:T(1,128)}), f32[8,1,2048]{2,1,0:T(1,128)S(1)}, u32[]{:S(2)}, u32[]{:S(2)}) %all-to-all-start.2) | async-done | bytes 65568 | tf_op jit(solution)/shard_map/all_to_all | solution.py:196
  107.1 4.9 %convolution_divide_fusion.1 = f32[32,512]{1,0:T(8,128)S(1)} fusion(f32[32,512]{1,0:T(8,128)S(1)} %all_to_all.71, s32[512]{0:T(512)S(1)} %multiply_add_fusion.1, f32[512]{0:T(512)S(1)} %fusion.88, f32[512]{0:T(512)S(1)} %multiply_multiply_fusion, f32[32]{0:T(128)S(1)} %multiply_multiply_fusion.1), kind=kOutput, calls=%fused_computation.9 | convolution fusion | flops 104644608 | bytes 137344 | tf_op jit(solution)/shard_map/dot_general | solution.py:62
  112.0 4.6 %fusion.21 = f32[32,512]{1,0:T(8,128)S(1)} fusion(f32[32,512]{1,0:T(8,128)S(1)} %convolution_divide_fusion.1, s32[512]{0:T(512)S(1)} %multiply_add_fusion.1, f32[512]{0:T(512)S(1)} %fusion.88), kind=kOutput, calls=%fused_computation.38 | convolution fusion | flops 104595456 | bytes 135168 | tf_op jit(solution)/shard_map/dot_general | solution.py:62
  121.1 6.5 %all-to-all-done.3 = f32[8,1,2048]{2,1,0:T(1,128)S(1)} async-done(((f32[8,1,2048]{2,1,0:T(1,128)}), f32[8,1,2048]{2,1,0:T(1,128)S(1)}, u32[]{:S(2)}, u32[]{:S(2)}) %all-to-all-start.3) | async-done | bytes 65568 | tf_op jit(solution)/shard_map/all_to_all | solution.py:199
  131.7 5.2 %reduce-scatter.7.cloned.1.call-done = f32[256,64]{0,1:T(8,128)} async-done(((f32[512,64]{0,1:T(8,128)}), f32[256,64]{0,1:T(8,128)}) %reduce-scatter.7.cloned.1.call-update) | async-done | bytes 65552 | tf_op jit(solution)/shard_map/reduce_scatter | solution.py:203
  154.0 32.5 %all-reduce.1 = (f32[]{:T(128)}, f32[]{:T(128)}) all-reduce(f32[]{:T(128)} %get-tuple-element.3, f32[]{:T(128)} %get-tuple-element.2), channel_id=1, replica_groups=mesh['pass'=2,'az'=8,'rg'=2] {'az','rg'}, use_global_device_ids=true, to_apply=%region_7.8 | all-reduce | flops 2 | bytes 16 | tf_op jit(solution)/shard_map/psum | solution.py:130
  191.2 5.0 %reduce-scatter.9.cloned.1.call-done = f32[256,64]{0,1:T(8,128)} async-done(((f32[512,64]{0,1:T(8,128)}), f32[256,64]{0,1:T(8,128)}) %reduce-scatter.9.cloned.1.call-update) | async-done | bytes 65552 | tf_op jit(solution)/shard_map/reduce_scatter | solution.py:193
  197.2 12.4 %all_to_all.90 = f32[8,1,2048]{2,1,0:T(1,128)S(1)} all-to-all(f32[8,1,2048]{2,1,0:T(1,128)S(1)} %reshape.190), channel_id=1, replica_groups=mesh['pass'=2,'az'=8,'rg'=2] {'az'}, dimensions={0} | all-to-all | bytes 131072 | tf_op jit(solution)/shard_map/all_to_all | solution.py:196
  210.7 4.9 %convolution_divide_fusion = f32[32,512]{1,0:T(8,128)S(1)} fusion(f32[32,512]{1,0:T(8,128)S(1)} %all_to_all.79, s32[512]{0:T(512)S(1)} %multiply_add_fusion.1, f32[512]{0:T(512)S(1)} %fusion.88, f32[512]{0:T(512)S(1)} %multiply_multiply_fusion, f32[32]{0:T(128)S(1)} %multiply_multiply_fusion.1), kind=kOutput, calls=%fused_computation.8 | convolution fusion | flops 104644608 | bytes 137344 | tf_op jit(solution)/shard_map/dot_general | solution.py:62
  215.6 4.6 %fusion.18 = f32[32,512]{1,0:T(8,128)S(1)} fusion(f32[32,512]{1,0:T(8,128)S(1)} %convolution_divide_fusion, s32[512]{0:T(512)S(1)} %multiply_add_fusion.1, f32[512]{0:T(512)S(1)} %fusion.88), kind=kOutput, calls=%fused_computation.37 | convolution fusion | flops 104595456 | bytes 135168 | tf_op jit(solution)/shard_map/dot_general | solution.py:62
  220.4 9.3 %all_to_all.91 = f32[8,1,2048]{2,1,0:T(1,128)S(1)} all-to-all(f32[8,1,2048]{2,1,0:T(1,128)S(1)} %reshape.192), channel_id=1, replica_groups=mesh['pass'=2,'az'=8,'rg'=2] {'az'}, dimensions={0} | all-to-all | bytes 131072 | tf_op jit(solution)/shard_map/all_to_all | solution.py:199
  233.7 5.2 %reduce-scatter.11.cloned.1.call-done = f32[256,64]{0,1:T(8,128)} async-done(((f32[512,64]{0,1:T(8,128)}), f32[256,64]{0,1:T(8,128)}) %reduce-scatter.11.cloned.1.call-update) | async-done | bytes 65552 | tf_op jit(solution)/shard_map/reduce_scatter | solution.py:203
  240.4 34.5 %psum.30 = f32[]{:T(128)} all-reduce(f32[]{:T(128)} %fusion.85), channel_id=1, replica_groups=mesh['pass'=2,'az'=8,'rg'=2] {'az','rg'}, use_global_device_ids=true, to_apply=%region_13.14 | all-reduce | flops 1 | bytes 8 | tf_op jit(solution)/shard_map/psum | solution.py:130
  278.3 4.5 %collective-permute-start.9 = (f32[1,256]{1,0:T(1,128)S(1)}, f32[1,256]{1,0:T(1,128)S(1)}, u32[]{:S(2)}, u32[]{:S(2)}) collective-permute-start(f32[1,256]{1,0:T(1,128)S(1)} %get-tuple-element.24), channel_id=1, source_target_pairs={{0,2},{2,4},{4,6},{6,8},{8,10},{10,12},{12,14},{1,3},{3,5},{5,7},{... | collective-permute-start | bytes 3080 | tf_op jit(solution)/shard_map/ppermute | solution.py:34
  289.4 30.3 %psum.31 = f32[]{:T(128)} all-reduce(f32[]{:T(128)} %get-tuple-element.6), channel_id=1, replica_groups=mesh['pass'=2,'az'=8,'rg'=2] {'az','rg'}, use_global_device_ids=true, to_apply=%region_15.16 | all-reduce | flops 1 | bytes 8 | tf_op jit(solution)/shard_map/psum | solution.py:217
  (114 shorter events, 72.7 us)
Async XLA Ops:
  9.5 23.6 %all-to-all-start = ((s32[1,8,16]{2,0,1:T(1,128)}), s32[1,8,16]{2,0,1:T(1,128)S(1)}, u32[]{:S(2)}, u32[]{:S(2)}) async-start(s32[1,8,16]{2,0,1:T(1,128)} %bitcast), calls=%async_computation | async-start | bytes 8192 | tf_op jit(solution)/shard_map/all_to_all | solution.py:157
  17.6 21.5 %copy-start.2 = (s32[64]{0:T(128)S(1)}, s32[64]{0:T(128)}, u32[]{:S(2)}) copy-start(s32[64]{0:T(128)} %param.10) | copy-start | bytes 772
  30.0 28.8 %copy-start.1 = (s32[64,256]{1,0:T(8,128)S(1)}, s32[64,256]{1,0:T(8,128)}, u32[]{:S(2)}) copy-start(s32[64,256]{1,0:T(8,128)} %param.11) | copy-start | bytes 196612
  33.1 20.0 %all-to-all-start.1 = ((f32[4,128,256]{2,0,1:T(4,128)}), f32[4,128,256]{2,0,1:T(4,128)S(1)}, u32[]{:S(2)}, u32[]{:S(2)}) async-start(f32[4,128,256]{2,0,1:T(4,128)} %select_bitcast_fusion), calls=%async_computation.1 | async-start | bytes 1048576 | tf_op jit(solution)/shard_map/all_to_all | solution.py:156
  39.1 52.2 %reduce-scatter.5.cloned.1.call-start = ((), (), s32[]{:S(2)}) async-start(), calls=%async_computation.10 | async-start | bytes 196608 | tf_op jit(solution)/shard_map/reduce_scatter | solution.py:193
  57.5 8.6 %collective-permute-start = (f32[4,64,256]{2,0,1:T(4,128)S(1)}, f32[4,64,256]{2,0,1:T(4,128)S(1)}, u32[]{:S(2)}, u32[]{:S(2)}) collective-permute-start(f32[4,64,256]{2,0,1:T(4,128)S(1)} %scatter_fusion), channel_id=1, source_target_pairs={{2,0},{4,2},{6,4},{8,6},{10,8},{12,10},{14,12},{3,1},{5,3},{7,5},{... | collective-permute-start | bytes 786440 | tf_op jit(solution)/shard_map/ppermute | solution.py:24
  67.2 5.9 %collective-permute-start.1 = (f32[3,1,256]{2,1,0:T(1,128)S(1)}, f32[3,1,256]{2,1,0:T(1,128)S(1)}, u32[]{:S(2)}, u32[]{:S(2)}) collective-permute-start(f32[3,1,256]{2,1,0:T(1,128)S(1)} %get-tuple-element.18), channel_id=1, source_target_pairs={{0,2},{2,4},{4,6},{6,8},{8,10},{10,12},{12,14},{1,3},{3,5},{5,7},{... | collective-permute-start | bytes 9224 | tf_op jit(solution)/shard_map/ppermute | solution.py:34
  71.7 5.5 %collective-permute-start.2 = (f32[3,1,256]{2,1,0:T(1,128)S(1)}, f32[3,1,256]{2,1,0:T(1,128)S(1)}, u32[]{:S(2)}, u32[]{:S(2)}) collective-permute-start(f32[3,1,256]{2,1,0:T(1,128)S(1)} %get-tuple-element.19), channel_id=1, source_target_pairs={{2,0},{4,2},{6,4},{8,6},{10,8},{12,10},{14,12},{3,1},{5,3},{7,5},{... | collective-permute-start | bytes 9224 | tf_op jit(solution)/shard_map/ppermute | solution.py:35
  77.3 2.6 collective-permute-start.3
  78.6 3.2 collective-permute-start.4
  92.9 12.6 %all-to-all-start.2 = ((f32[8,1,2048]{2,1,0:T(1,128)}), f32[8,1,2048]{2,1,0:T(1,128)S(1)}, u32[]{:S(2)}, u32[]{:S(2)}) async-start(f32[8,1,2048]{2,1,0:T(1,128)} %reshape.186), calls=%async_computation.3 | async-start | bytes 131072 | tf_op jit(solution)/shard_map/all_to_all | solution.py:196
  117.5 10.2 %all-to-all-start.3 = ((f32[8,1,2048]{2,1,0:T(1,128)}), f32[8,1,2048]{2,1,0:T(1,128)S(1)}, u32[]{:S(2)}, u32[]{:S(2)}) async-start(f32[8,1,2048]{2,1,0:T(1,128)} %reshape.188), calls=%async_computation.4 | async-start | bytes 131072 | tf_op jit(solution)/shard_map/all_to_all | solution.py:199
  120.8 16.1 %reduce-scatter.7.cloned.1.call-start = ((), (), s32[]{:S(2)}) async-start(), calls=%async_computation.11 | async-start | bytes 196608 | tf_op jit(solution)/shard_map/reduce_scatter | solution.py:203
  131.7 64.5 %reduce-scatter.9.cloned.1.call-start = ((), (), s32[]{:S(2)}) async-start(), calls=%async_computation.12 | async-start | bytes 196608 | tf_op jit(solution)/shard_map/reduce_scatter | solution.py:193
  137.6 4.9 %collective-permute-start.5 = (f32[1,256]{1,0:T(1,128)S(1)}, f32[1,256]{1,0:T(1,128)S(1)}, u32[]{:S(2)}, u32[]{:S(2)}) collective-permute-start(f32[1,256]{1,0:T(1,128)S(1)} %get-tuple-element.26), channel_id=1, source_target_pairs={{0,2},{2,4},{4,6},{6,8},{8,10},{10,12},{12,14},{1,3},{3,5},{5,7},{... | collective-permute-start | bytes 3080 | tf_op jit(solution)/shard_map/ppermute | solution.py:34
  141.2 5.5 %collective-permute-start.6 = (f32[1,256]{1,0:T(1,128)S(1)}, f32[1,256]{1,0:T(1,128)S(1)}, u32[]{:S(2)}, u32[]{:S(2)}) collective-permute-start(f32[1,256]{1,0:T(1,128)S(1)} %get-tuple-element.27), channel_id=1, source_target_pairs={{2,0},{4,2},{6,4},{8,6},{10,8},{12,10},{14,12},{3,1},{5,3},{7,5},{... | collective-permute-start | bytes 3080 | tf_op jit(solution)/shard_map/ppermute | solution.py:35
  147.6 2.6 collective-permute-start.7
  148.9 3.1 collective-permute-start.8
  191.1 47.8 %reduce-scatter.11.cloned.1.call-start = ((), (), s32[]{:S(2)}) async-start(), calls=%async_computation.13 | async-start | bytes 196608 | tf_op jit(solution)/shard_map/reduce_scatter | solution.py:203
  215.6 60.6 %copy-start = (f32[256,64]{0,1:T(8,128)S(1)}, f32[256,64]{0,1:T(8,128)}, u32[]{:S(2)}) copy-start(f32[256,64]{0,1:T(8,128)} %reduce-scatter.7.cloned.1.call-done) | copy-start | bytes 196612
  277.0 5.9 %collective-permute-start.10 = (f32[1,256]{1,0:T(1,128)S(1)}, f32[1,256]{1,0:T(1,128)S(1)}, u32[]{:S(2)}, u32[]{:S(2)}) collective-permute-start(f32[1,256]{1,0:T(1,128)S(1)} %get-tuple-element.25), channel_id=1, source_target_pairs={{2,0},{4,2},{6,4},{8,6},{10,8},{12,10},{14,12},{3,1},{5,3},{7,5},{... | collective-permute-start | bytes 3080 | tf_op jit(solution)/shard_map/ppermute | solution.py:35
  278.3 5.8 %collective-permute-start.9 = (f32[1,256]{1,0:T(1,128)S(1)}, f32[1,256]{1,0:T(1,128)S(1)}, u32[]{:S(2)}, u32[]{:S(2)}) collective-permute-start(f32[1,256]{1,0:T(1,128)S(1)} %get-tuple-element.24), channel_id=1, source_target_pairs={{0,2},{2,4},{4,6},{6,8},{8,10},{10,12},{12,14},{1,3},{3,5},{5,7},{... | collective-permute-start | bytes 3080 | tf_op jit(solution)/shard_map/ppermute | solution.py:34
  284.3 2.6 collective-permute-start.11
  285.6 3.1 collective-permute-start.12
Sparse Core Ops, SparseCore 0:
  85.5 5.6 reduce-scatter.4
  131.8 5.0 reduce-scatter.6
  191.2 4.8 reduce-scatter.8
  233.8 5.0 reduce-scatter.10

commit v2 on v1

--- a/solution.py
+++ b/solution.py
@@ -126,6 +126,474 @@
     )(ref_lines, sec_lines, group, line_of)
 
 
+class Exchange:
+    def __init__(self, send_sems, recv_sems):
+        self.send_sems, self.recv_sems = send_sems, recv_sems
+        self.used = 0
+
+    def copy(self, source, target, device):
+        index = self.used
+        self.used += 1
+        return pltpu.make_async_remote_copy(
+            src_ref=source,
+            dst_ref=target,
+            send_sem=self.send_sems.at[index],
+            recv_sem=self.recv_sems.at[index],
+            device_id=device,
+            device_id_type=pl.DeviceIdType.MESH,
+        )
+
+
+def full_dot(left, right, dims=(1, 0)):
+    return lax.dot_general(
+        left,
+        right,
+        (((dims[0],), (dims[1],)), ((), ())),
+        precision=FULL_PRECISION,
+        preferred_element_type=jnp.float32,
+    )
+
+
+def iota(shape, dim):
+    return lax.broadcasted_iota(jnp.int32, shape, dim)
+
+
+def unwrap_kernel(
+    peers,
+    capacity,
+    damping,
+    sums_ref,
+    target_row_ref,
+    target_col_ref,
+    seam_ref,
+    mask_ref,
+    basis_ref,
+    lam_row_ref,
+    lam_col_ref,
+    out_ref,
+    res_ref,
+    slot_send,
+    slot_recv,
+    place_send,
+    place_recv,
+    grid_own,
+    grid_next,
+    fields,
+    spec_send,
+    spec_recv,
+    back_send,
+    back_recv,
+    dot_send,
+    dot_recv,
+    send_sems,
+    recv_sems,
+):
+    me = lax.axis_index("az")
+    core = lax.axis_index("rg")
+    other = 1 - core
+    last = peers - 1
+    rows, cols = mask_ref.shape
+    length = basis_ref.shape[0]
+    slots = peers * capacity
+    pencil = cols // peers
+    exchange = Exchange(send_sems, recv_sems)
+    sent = []
+
+    def at(az, rg):
+        return (lax.axis_index("pass"), az, rg)
+
+    def ahead(offset):
+        return lax.rem(me + offset, peers)
+
+    def behind(offset):
+        return lax.rem(me + peers - offset, peers)
+
+    barrier = pltpu.get_barrier_semaphore()
+    for offset in range(peers):
+        for side in (core, other):
+            if offset or side is other:
+                pl.semaphore_signal(
+                    barrier,
+                    inc=1,
+                    device_id=at(ahead(offset), side),
+                    device_id_type=pl.DeviceIdType.MESH,
+                )
+
+    target_row = target_row_ref[...]
+    target_col = target_col_ref[...]
+    owner_row = target_row // rows
+    owner_col = target_col // rows
+    same = owner_col == owner_row
+    low_index = iota((rows, rows), 0)
+    high_index = iota((rows, rows), 1)
+    rank_row = jnp.sum(
+        jnp.where(same & (low_index < high_index), 1, 0), axis=0, keepdims=True
+    )
+    rank_col = jnp.sum(
+        jnp.where(same & (high_index < low_index), 1, 0), axis=1, keepdims=True
+    )
+    choose = jnp.where(
+        iota((slots, rows), 0) == owner_row * capacity + rank_row, 1.0, 0.0
+    ).astype(jnp.float32)
+    place = (target_col - owner_col * rows + 1).astype(jnp.float32)
+    lane = iota((rows, slots), 1)
+    here = lane == me * capacity + rank_col
+    for dest in range(peers):
+        line = jnp.sum(
+            jnp.where(here & (owner_col == dest), place, 0.0), axis=0, keepdims=True
+        )
+        place_send[dest] = jnp.broadcast_to(line, (8, slots))
+    for plane in range(4):
+        chosen = full_dot(choose, sums_ref[plane])
+        slot_send[plane] = chosen.reshape(peers, capacity, cols)
+
+    pl.semaphore_wait(barrier, 2 * peers - 1)
+    place_copies = []
+    for offset in range(1, peers):
+        copy = exchange.copy(
+            place_send.at[ahead(offset)], place_recv.at[me], at(ahead(offset), core)
+        )
+        copy.start()
+        place_copies.append(copy)
+    slot_copies = []
+    for plane in range(4):
+        row_copies = []
+        for offset in range(1, peers):
+            copy = exchange.copy(
+                slot_send.at[plane, ahead(offset)],
+                slot_recv.at[plane, me],
+                at(ahead(offset), core),
+            )
+            copy.start()
+            row_copies.append(copy)
+        slot_copies.append(row_copies)
+        slot_recv[plane, me] = slot_send[plane, me]
+        sent += row_copies
+    place_recv[me] = place_send[me]
+    sent += place_copies
+
+    seam_pick = jnp.where(seam_ref[...] == iota((rows, rows), 1), 1.0, 0.0).astype(jnp.float32)
+    for copy in place_copies:
+        copy.wait_recv()
+    places = place_recv[0]
+    for source in range(1, peers):
+        places = places + place_recv[source]
+    scatter = jnp.where(
+        places[0:1] == (iota((rows, slots), 0) + 1).astype(jnp.float32), 1.0, 0.0
+    ).astype(jnp.float32)
+    seam_copies = []
+
+    @pl.when(me == last)
+    def _():
+        grid_next[...] = jnp.zeros_like(grid_next)
+
+    for plane in range(4):
+        for copy in slot_copies[plane]:
+            copy.wait_recv()
+        grid_own[plane] = full_dot(scatter, slot_recv[plane].reshape(slots, cols))
+        copy = exchange.copy(grid_own.at[plane], grid_next.at[plane], at(behind(1), core))
+
+        @pl.when(me > 0)
+        def _():
+            copy.start()
+
+        seam_copies.append(copy)
+
+    own_lanes = pl.ds(pl.multiple_of(core * cols, cols), cols)
+    fields[2, 8 : 8 + rows, own_lanes] = (1 + mask_ref[...]).astype(jnp.float32) * 0.25
+    combined = []
+    for plane in range(4):
+
+        @pl.when(me < last)
+        def _():
+            seam_copies[plane].wait_recv()
+
+        combined.append(grid_own[plane] + full_dot(seam_pick, grid_next[plane]))
+    magnitude = jnp.sqrt(combined[2] * combined[3]) + EPSILON
+    fields[0, 8 : 8 + rows, own_lanes] = combined[0] / magnitude
+    fields[1, 8 : 8 + rows, own_lanes] = combined[1] / magnitude
+
+    @pl.when(me == 0)
+    def _():
+        fields[:, 0:8, :] = jnp.zeros((3, 8, length), jnp.float32)
+
+    @pl.when(me == last)
+    def _():
+        fields[:, 8 + rows :, :] = jnp.zeros((3, 8, length), jnp.float32)
+
+    up_copies, down_copies = [], []
+    for side in (core, other):
+        up_copies.append(
+            exchange.copy(
+                fields.at[:, pl.ds(8, 8), own_lanes],
+                fields.at[:, pl.ds(8 + rows, 8), own_lanes],
+                at(behind(1), side),
+            )
+        )
+        down_copies.append(
+            exchange.copy(
+                fields.at[:, pl.ds(rows, 8), own_lanes],
+                fields.at[:, pl.ds(0, 8), own_lanes],
+                at(ahead(1), side),
+            )
+        )
+
+    @pl.when(me > 0)
+    def _():
+        for copy in up_copies:
+            copy.start()
+
+    @pl.when(me < last)
+    def _():
+        for copy in down_copies:
+            copy.start()
+
+    across = exchange.copy(
+        fields.at[:, pl.ds(8, rows), own_lanes],
+        fields.at[:, pl.ds(8, rows), own_lanes],
+        at(me, other),
+    )
+    across.start()
+    across.wait_recv()
+    sent.append(across)
+
+    @pl.when(me < last)
+    def _():
+        for copy in up_copies:
+            copy.wait_recv()
+
+    @pl.when(me > 0)
+    def _():
+        for copy in down_copies:
+            copy.wait_recv()
+
+    column = iota((rows, length), 1)
+
+    def beside(values):
+        middle = values[8 : 8 + rows]
+        return (
+            values[7 : 7 + rows],
+            values[9 : 9 + rows],
+            pltpu.roll(middle, 1, 1),
+            pltpu.roll(middle, length - 1, 1),
+        )
+
+    weight = fields[2]
+    inside = weight[8 : 8 + rows]
+    edges = [inside * item for item in beside(weight)]
+    edges[2] = jnp.where(column > 0, edges[2], 0.0)
+    edges[3] = jnp.where(column < length - 1, edges[3], 0.0)
+    real, imag = fields[0], fields[1]
+    right_side = jnp.zeros((rows, length), jnp.float32)
+    for edge, real_item, imag_item in zip(edges, beside(real), beside(imag)):
+        right_side = right_side + edge * (
+            imag[8 : 8 + rows] * real_item - real[8 : 8 + rows] * imag_item
+        )
+
+    def operator(values):
+        middle = values[8 : 8 + rows]
+        result = damping * middle
+        for edge, item in zip(edges, beside(values)):
+            result = result + edge * (middle - item)
+        return result
+
+    first_freq = pl.multiple_of(core * cols + me * pencil, pencil)
+    divisor = lam_col_ref[pl.ds(first_freq, pencil), :] + lam_row_ref[...] + damping
+
+    def gather_dots(turn, values):
+        row = iota((8, 128), 0)
+        tile = jnp.zeros((8, 128), jnp.float32)
+        for index, value in enumerate(values):
+            tile = jnp.where(row == index, jnp.sum(value, keepdims=True), tile)
+        dot_send[turn] = tile
+        dot_recv[turn, me] = tile
+        copies = []
+        for offset in range(1, peers):
+            copy = exchange.copy(
+                dot_send.at[turn], dot_recv.at[turn, me], at(ahead(offset), core)
+            )
+            copy.start()
+            copies.append(copy)
+        sent.extend(copies)
+
+        def finish():
+            for copy in copies:
+                copy.wait_recv()
+            total = dot_recv[turn, 0]
+            for source in range(1, peers):
+                total = total + dot_recv[turn, source]
+            return [total[index : index + 1, 0:1] for index in range(len(values))]
+
+        return finish
+
+    def precondition(turn, values, meanwhile):
+        half_basis = basis_ref[pl.ds(pl.multiple_of(core * cols, cols), cols), :]
+        spectrum = full_dot(half_basis, values, (1, 1))
+        half = pencil // 2
+        for dest in range(peers):
+            base = dest * pencil
+            spec_send[turn, dest] = jnp.concatenate(
+                [spectrum[base : base + half], spectrum[base + half : base + pencil]], axis=1
+            )
+        copies = []
+        for offset in range(1, peers):
+            copy = exchange.copy(
+                spec_send.at[turn, ahead(offset)],
+                spec_recv.at[turn, me],
+                at(ahead(offset), core),
+            )
+            copy.start()
+            copies.append(copy)
+        spec_recv[turn, me] = spec_send[turn, me]
+        extra = meanwhile()
+        for copy in copies:
+            copy.wait_recv()
+        sent.extend(copies)
+        blocks = [spec_recv[turn, source] for source in range(peers)]
+        columns = jnp.concatenate(
+            [
+                jnp.concatenate([block[:, :rows] for block in blocks], axis=1),
+                jnp.concatenate([block[:, rows:] for block in blocks], axis=1),
+            ],
+            axis=0,
+        )
+        filtered = full_dot(columns, basis_ref[...], (1, 1)) / divisor
+        restored = full_dot(filtered, basis_ref[...])
+        margin = jnp.zeros((pencil, rows // 2), jnp.float32)
+        padded = jnp.concatenate([margin, restored, margin], axis=1)
+        for dest in range(peers):
+            back_send[turn, dest] = padded[:, dest * rows : (dest + 2) * rows]
+        copies = []
+        for offset in range(1, peers):
+            copy = exchange.copy(
+                back_send.at[turn, ahead(offset)],
+                back_recv.at[turn, core, me],
+                at(ahead(offset), core),
+            )
+            copy.start()
+            copies.append(copy)
+        back_recv[turn, core, me] = back_send[turn, me]
+        relays = [
+            exchange.copy(
+                back_send.at[turn, me], back_recv.at[turn, core, me], at(me, other)
+            )
+        ]
+        relays[0].start()
+        for offset in range(1, peers):
+            copies[offset - 1].wait_recv()
+            held = back_recv.at[turn, core, behind(offset)]
+            relay = exchange.copy(held, held, at(me, other))
+            relay.start()
+            relays.append(relay)
+        for relay in relays:
+            relay.wait_recv()
+        sent.extend(copies + relays)
+        window = back_recv[turn].reshape(length, 2 * rows).T
+        start = rows // 2 - 8
+        return full_dot(window[start : start + rows + 16], basis_ref[...]), extra
+
+    z0, _ = precondition(0, right_side, lambda: None)
+    z0_mid = z0[8 : 8 + rows]
+    w0 = operator(z0)
+    y0, finish = precondition(
+        1, w0, lambda: gather_dots(0, [right_side * z0_mid, z0_mid * w0])
+    )
+    rho0, energy0 = finish()
+    alpha0 = rho0 / energy0
+    r1 = right_side - alpha0 * w0
+    z1 = z0 - alpha0 * y0
+    z1_mid = z1[8 : 8 + rows]
+    q1 = operator(z1)
+    rho1, energy1, cross = gather_dots(1, [r1 * z1_mid, z1_mid * q1, z0_mid * q1])()
+    beta = rho1 / rho0
+    alpha1 = rho1 / (energy1 + 2.0 * beta * cross + beta * beta * energy0)
+    answer = alpha0 * z0_mid + alpha1 * (z1_mid + beta * z0_mid)
+    left = r1 - alpha1 * (q1 + beta * w0)
+    out_ref[...] = jnp.where(core == 0, answer[:, :cols], answer[:, cols:])
+    res_ref[...] = jnp.where(core == 0, left[:, :cols], left[:, cols:])
+
+    for copy in sent:
+        copy.wait_send()
+
+    @pl.when(me > 0)
+    def _():
+        for copy in seam_copies + up_copies:
+            copy.wait_send()
+
+    @pl.when(me < last)
+    def _():
+        for copy in down_copies:
+            copy.wait_send()
+
+
+def fits_kernel(peers, cores, rows, cols):
+    length = rows * peers
+    capacity = max(2, 2 * rows // peers)
+    return (
+        cores == 2
+        and rows == 64
+        and length == cols * cores
+        and length <= 1024
+        and peers * capacity == 128
+        and cols % (16 * peers) == 0
+    )
+
+
+def unwrap_in_kernel(sums, line_target, seam_partner, mask_level, peers):
+    rows, cols = mask_level.shape
+    length = rows * peers
+    capacity = max(2, 2 * rows // peers)
+    damping = 0.25 / (rows * rows)
+    freq = np.arange(length)
+    angle = (2 * freq[None, :] + 1) * freq[:, None] % (4 * length)
+    basis = np.sqrt(np.where(freq == 0, 1.0, 2.0) / length)[:, None] * np.cos(
+        angle * (math.pi / (2.0 * length))
+    )
+    lam = 4.0 * np.sin(freq * (math.pi / (2.0 * length))) ** 2
+    pencil = cols // peers
+    copies = 4 * (peers - 1) + (peers - 1) + 4 + 5 + 2 * (3 * (peers - 1) + 1) + 2 * (peers - 1)
+    vmem = pl.BlockSpec(memory_space=pltpu.VMEM)
+    shape = jax.ShapeDtypeStruct((rows, cols), jnp.float32)
+
+    def scratch(*dims):
+        return pltpu.VMEM(dims, jnp.float32)
+
+    return pl.pallas_call(
+        functools.partial(unwrap_kernel, peers, capacity, damping),
+        out_shape=(shape, shape),
+        in_specs=[vmem] * 8,
+        out_specs=(vmem, vmem),
+        scratch_shapes=[
+            scratch(4, peers, capacity, cols),
+            scratch(4, peers, capacity, cols),
+            scratch(peers, 8, 128),
+            scratch(peers, 8, 128),
+            scratch(4, rows, cols),
+            scratch(4, rows, cols),
+            scratch(3, rows + 16, length),
+            scratch(2, peers, pencil // 2, 2 * rows),
+            scratch(2, peers, pencil // 2, 2 * rows),
+            scratch(2, peers, pencil, 2 * rows),
+            scratch(2, 2, peers, pencil, 2 * rows),
+            scratch(2, 8, 128),
+            scratch(2, peers, 8, 128),
+            pltpu.SemaphoreType.DMA((copies,)),
+            pltpu.SemaphoreType.DMA((copies,)),
+        ],
+        compiler_params=pltpu.CompilerParams(collective_id=0, has_side_effects=True),
+        name="unwrap",
+    )(
+        sums,
+        line_target.reshape(1, rows),
+        line_target.reshape(rows, 1),
+        seam_partner.reshape(rows, 1),
+        mask_level,
+        basis.astype(np.float32),
+        lam.astype(np.float32)[None, :],
+        lam.astype(np.float32)[:, None],
+    )
+
+
 def single_product(left, right):
     return lax.psum(jnp.sum(left * right), ("az", "rg"))
 
@@ -137,6 +605,9 @@
     rg_place = lax.axis_index("rg")
     row_count = line_target.shape[0]
     col_count = mask_level.shape[1]
+    local_sums = form_looks(reference_slc, secondary_slc, col_count)
+    if fits_kernel(dev_count, rg_count, row_count, col_count):
+        return unwrap_in_kernel(local_sums, line_target, seam_partner, mask_level, dev_count)
     capacity = max(2, 2 * row_count // dev_count)
     owners = line_target // row_count
     local_index = jnp.arange(row_count, dtype=jnp.int32)
@@ -150,7 +621,6 @@
         .at[0, slot_index]
         .set(line_target % row_count)
     )
-    local_sums = form_looks(reference_slc, secondary_slc, col_count)
     sent_sums = jnp.take(local_sums, source_row, axis=1, mode="fill", fill_value=0.0)
     got_sums, got_positions = (
         lax.all_to_all(sent_sums, "az", split_axis=1, concat_axis=1, tiled=True),

time: 330 us -> 83.5 us (0.25)
  blocking collectives: 119 us -> 0 us
  waiting for transfers between devices: 69.6 us -> 0 us
  Pallas kernels: 12.4 us -> 76.7 us
  starting transfers between devices: 48.3 us -> 0 us
  matrix products: 31.7 us -> 0 us
  between operations: 18.3 us -> 0.64 us
  other arithmetic: 13 us -> 0 us
  local copies, waits for them, and re-layouts: 16.1 us -> 5.66 us
    psum x3 -> x0, blocking collectives: 97.2 us -> none  [the longest x2 67 us: single_product(): return lax.psum(jnp.sum(left * right), ('az', 'rg'))]
    pallas_call x0 -> x1, Pallas kernels: none -> 64.3 us  [unwrap_in_kernel(): pl.pallas_call(functools.partial(unwrap_kernel, peers, capacity, damping)...]
    dot_general x8 -> x0, matrix products: 31.7 us -> none  [contract(): lax.dot_general(left, right, (((left_dim,), (right_dim,)), ((), ())), pre...]
    all_to_all x4 -> x0, waiting for transfers between devices: 26 us -> none  [the longest x1 12.6 us: on_device(): lax.all_to_all(sent_sums, 'az', split_axis=1, concat_axis=1, tiled=True)]
    ppermute x13 -> x0, starting transfers between devices: 25.5 us -> none  [the longest x6 16.5 us: with_halo(): before = lax.ppermute(last, axis, up)]
    ppermute x13 -> x0, waiting for transfers between devices: 22.4 us -> none  [the longest x6 13.8 us: with_halo(): after = lax.ppermute(first, axis, down)]
    all_to_all x4 -> x0, starting transfers between devices: 22.3 us -> none  [the longest x1 7.28 us: on_device(): lax.all_to_all(positions, 'az', split_axis=1, concat_axis=1, tiled=True)]
    all_to_all x2 -> x0, blocking collectives: 21.7 us -> none  [the longest x1 12.4 us: precondition(): lax.all_to_all(range_spectrum, 'az', split_axis=0, concat_axis=1, tiled=T...]
  transfers between devices with their start and end apart: 21 -> 0, of which waited for: 14 -> 0; matrix products, arithmetic and copies ran while one was open for 2% -> 0% of each run, Pallas kernels for 4% -> 0%
where the time goes in v2:
time: 83.5 us; the launch traced here: 83 us
  Pallas kernels  76.7 us (92%)
  local copies, waits for them, and re-layouts  5.66 us (7%)
    pallas_call x1, Pallas kernels, unwrap_in_kernel(): pl.pallas_call(functools.partial(unwrap_kernel, peers, capacity, damping)...  64.3 us
    pallas_call x1, Pallas kernels, form_looks(): pl.pallas_call(functools.partial(look_kernel, lines, half), grid=(line_co...  12.4 us
    unnamed x2, local copies, waits for them, and re-layouts  2.95 us

profile of v2, /device:TPU:0, one launch (start us, length us, event | category | flops | bytes accessed | tf_op | source)
XLA Modules:
  0.0 83.0 jit_solution(4792197963421805603)
XLA Ops:
  0.6 1.4 %copy.13.seam_ref = s32[64,1]{1,0:T(8,128)} copy(s32[64,1]{0,1:T(1,128)} %bitcast.5) | data formatting | bytes 512 | tf_op jit(solution)/shard_map/reshape | solution.py:589
  2.0 1.4 %copy.12.target_col_ref = s32[64,1]{1,0:T(8,128)} copy(s32[64,1]{0,1:T(1,128)} %bitcast.3) | data formatting | bytes 512 | tf_op jit(solution)/shard_map/reshape | solution.py:588
  3.3 12.4 %form_looks.1.sums_ref = f32[4,64,256]{2,1,0:T(8,128)} custom-call(bf16[2,256,5120]{2,1,0:T(8,128)(2,1)} %ref_ref.1, bf16[2,256,5120]{2,1,0:T(8,128)(2,1)} %sec_ref.1, bf16[2560,128]{1,0:T(8,128)(2,1)} %constant.10.clone.group_ref, f32[32,128]{1,0:T(8,128)} %constant.11.clone.line_ref), custom_call_target="tpu_custom_call" | custom-call | tf_op jit(solution)/shard_map/form_looks/pallas_call | solution.py:114
  15.7 64.3 %unwrap.1 = (f32[64,256]{1,0:T(8,128)}, f32[64,256]{1,0:T(8,128)}) custom-call(f32[4,64,256]{2,1,0:T(8,128)} %form_looks.1.sums_ref, s32[1,64]{1,0:T(1,128)} %bitcast.4, s32[64,1]{1,0:T(8,128)} %copy.12.target_col_ref, s32[64,1]{1,0:T(8,128)} %copy.13.seam_ref, s32[64,256]{1,0:T(8,128)} %mask_ref.1, f32[512,512]{1,0:T(8,128)} %constant.12.clone.basis_ref, ...), custom_call_target="tpu_custom_call" | custom-call | tf_op jit(solution)/shard_map/unwrap/pallas_call | solution.py:561
  80.1 1.5 %copy.16 = f32[64,256]{1,0:T(8,128)} copy(f32[64,256]{1,0:T(8,128)} %get-tuple-element.4) | data formatting | bytes 131072
  81.5 1.5 %copy.17 = f32[64,256]{1,0:T(8,128)} copy(f32[64,256]{1,0:T(8,128)} %get-tuple-element.5) | data formatting | bytes 131072

commit v3 on v2

--- a/solution.py
+++ b/solution.py
@@ -144,14 +144,71 @@
         )
 
 
-def full_dot(left, right, dims=(1, 0)):
+def split(values):
+    high = values.astype(jnp.bfloat16)
+    rest = values - high.astype(jnp.float32)
+    middle = rest.astype(jnp.bfloat16)
+    return high, middle, (rest - middle.astype(jnp.float32)).astype(jnp.bfloat16)
+
+
+def narrow_dot(left, right, dim):
     return lax.dot_general(
-        left,
-        right,
-        (((dims[0],), (dims[1],)), ((), ())),
-        precision=FULL_PRECISION,
-        preferred_element_type=jnp.float32,
-    )
+        left, right, (((1,), (dim,)), ((), ())), preferred_element_type=jnp.float32
+    )
+
+
+def pick_dot(choose, values):
+    high, middle, low = [narrow_dot(choose, part, 0) for part in split(values)]
+    return high + (middle + low)
+
+
+def basis_dot(values, basis, dim):
+    count = values.shape[0]
+    high, middle, low = split(values)
+    first = narrow_dot(jnp.concatenate([high, middle, low], axis=0), basis[0], dim)
+    second = narrow_dot(jnp.concatenate([high, middle], axis=0), basis[1], dim)
+    third = narrow_dot(high, basis[2], dim)
+    small = first[2 * count :] + second[count:] + third
+    return first[:count] + ((first[count : 2 * count] + second[:count]) + small)
+
+
+LINES = 64
+
+
+def form_block(index, width, ref_held, sec_held, group_ref, hold, looks):
+    step_rows = LINES // LOOK_AZ
+    lines = pl.ds(index * LINES, LINES)
+    total = jnp.zeros((8 * step_rows, width), jnp.float32)
+    for start in range(0, ref_held.shape[2], CHUNK):
+        parts = []
+        for begin in range(start, start + CHUNK, 128):
+            span = pl.ds(begin, 128)
+            slot = begin // 128
+            mr = ref_held[0, lines, span].astype(jnp.float32)
+            mi = ref_held[1, lines, span].astype(jnp.float32)
+            sr = sec_held[0, lines, span].astype(jnp.float32)
+            si = sec_held[1, lines, span].astype(jnp.float32)
+            hold[slot, 0:LINES] = mr * sr + mi * si
+            hold[slot, LINES : 2 * LINES] = mi * sr - mr * si
+            hold[slot, 2 * LINES : 3 * LINES] = mr * mr + mi * mi
+            hold[slot, 3 * LINES :] = sr * sr + si * si
+            part = hold[slot, pl.ds(0, 4 * step_rows, stride=LOOK_AZ), :]
+            for line in range(1, LOOK_AZ):
+                part = part + hold[slot, pl.ds(line, 4 * step_rows, stride=LOOK_AZ), :]
+            parts.append(part)
+        sums = jnp.concatenate(parts, axis=1)
+        high = sums.astype(jnp.bfloat16)
+        low = (sums - high.astype(jnp.float32)).astype(jnp.bfloat16)
+        total = total + jnp.dot(
+            jnp.concatenate([high, low], axis=0),
+            group_ref[pl.ds(start, CHUNK), :],
+            preferred_element_type=jnp.float32,
+        )
+    joined = total[: 4 * step_rows] + total[4 * step_rows :]
+    for plane in range(4):
+        looks[plane, pl.ds(index * step_rows, step_rows), :] = joined[
+            plane * step_rows : (plane + 1) * step_rows
+        ]
 
 
 def iota(shape, dim):
@@ -162,16 +219,21 @@
     peers,
     capacity,
     damping,
-    sums_ref,
-    target_row_ref,
-    target_col_ref,
-    seam_ref,
+    ref_ref,
+    sec_ref,
+    group_ref,
+    target_ref,
+    seam_row_ref,
     mask_ref,
     basis_ref,
     lam_row_ref,
     lam_col_ref,
     out_ref,
-    res_ref,
+    ref_held,
+    sec_held,
+    hold,
+    looks,
+    load_sems,
     slot_send,
     slot_recv,
     place_send,
@@ -193,7 +255,7 @@
     other = 1 - core
     last = peers - 1
     rows, cols = mask_ref.shape
-    length = basis_ref.shape[0]
+    length = basis_ref.shape[1]
     slots = peers * capacity
     pencil = cols // peers
     exchange = Exchange(send_sems, recv_sems)
@@ -207,6 +269,20 @@
 
     def behind(offset):
         return lax.rem(me + peers - offset, peers)
+
+    half = ref_held.shape[3]
+    width = half // LOOK_RG
+    blocks = rows * LOOK_AZ // LINES
+    loads = {}
+    for side in range(2):
+        for index in range(blocks):
+            for which, (source, target) in enumerate(((ref_ref, ref_held), (sec_ref, sec_held))):
+                loads[side, index, which] = pltpu.make_async_copy(
+                    source.at[:, pl.ds(index * LINES, LINES), pl.ds(side * half, half)],
+                    target.at[side, :, pl.ds(index * LINES, LINES), :],
+                    load_sems.at[side, index, which],
+                )
+                loads[side, index, which].start()
 
     barrier = pltpu.get_barrier_semaphore()
     for offset in range(peers):
@@ -219,8 +295,12 @@
                     device_id_type=pl.DeviceIdType.MESH,
                 )
 
-    target_row = target_row_ref[...]
-    target_col = target_col_ref[...]
+    def upright(line):
+        diagonal = iota((rows, rows), 0) == iota((rows, rows), 1)
+        return jnp.sum(jnp.where(diagonal, line, 0), axis=1, keepdims=True)
+
+    target_row = target_ref[...]
+    target_col = upright(target_row)
     owner_row = target_row // rows
     owner_col = target_col // rows
     same = owner_col == owner_row
@@ -234,7 +314,7 @@
     )
     choose = jnp.where(
         iota((slots, rows), 0) == owner_row * capacity + rank_row, 1.0, 0.0
-    ).astype(jnp.float32)
+    ).astype(jnp.bfloat16)
     place = (target_col - owner_col * rows + 1).astype(jnp.float32)
     lane = iota((rows, slots), 1)
     here = lane == me * capacity + rank_col
@@ -243,10 +323,6 @@
             jnp.where(here & (owner_col == dest), place, 0.0), axis=0, keepdims=True
         )
         place_send[dest] = jnp.broadcast_to(line, (8, slots))
-    for plane in range(4):
-        chosen = full_dot(choose, sums_ref[plane])
-        slot_send[plane] = chosen.reshape(peers, capacity, cols)
-
     pl.semaphore_wait(barrier, 2 * peers - 1)
     place_copies = []
     for offset in range(1, peers):
@@ -255,24 +331,36 @@
         )
         copy.start()
         place_copies.append(copy)
+    place_recv[me] = place_send[me]
+    sent += place_copies
     slot_copies = []
-    for plane in range(4):
-        row_copies = []
+    for side in range(2):
+        for index in range(blocks):
+            loads[side, index, 0].wait()
+            loads[side, index, 1].wait()
+            form_block(index, width, ref_held.at[side], sec_held.at[side], group_ref, hold, looks.at[side])
+        joined = jnp.concatenate([looks[side, plane] for plane in range(4)], axis=1)
+        chosen = pick_dot(choose, joined)
+        for plane in range(4):
+            slot_send[side, :, plane] = chosen[:, plane * width : (plane + 1) * width].reshape(
+                peers, capacity, width
+            )
+        side_copies = []
         for offset in range(1, peers):
             copy = exchange.copy(
-                slot_send.at[plane, ahead(offset)],
-                slot_recv.at[plane, me],
+                slot_send.at[side, ahead(offset)],
+                slot_recv.at[side, me],
                 at(ahead(offset), core),
             )
             copy.start()
-            row_copies.append(copy)
-        slot_copies.append(row_copies)
-        slot_recv[plane, me] = slot_send[plane, me]
-        sent += row_copies
-    place_recv[me] = place_send[me]
-    sent += place_copies
-
-    seam_pick = jnp.where(seam_ref[...] == iota((rows, rows), 1), 1.0, 0.0).astype(jnp.float32)
+            side_copies.append(copy)
+        slot_recv[side, me] = slot_send[side, me]
+        slot_copies.append(side_copies)
+        sent += side_copies
+
+    seam_pick = jnp.where(
+        upright(seam_row_ref[...]) == iota((rows, rows), 1), 1.0, 0.0
+    ).astype(jnp.bfloat16)
     for copy in place_copies:
         copy.wait_recv()
     places = place_recv[0]
@@ -280,18 +368,24 @@
         places = places + place_recv[source]
     scatter = jnp.where(
         places[0:1] == (iota((rows, slots), 0) + 1).astype(jnp.float32), 1.0, 0.0
-    ).astype(jnp.float32)
+    ).astype(jnp.bfloat16)
     seam_copies = []
 
     @pl.when(me == last)
     def _():
         grid_next[...] = jnp.zeros_like(grid_next)
 
-    for plane in range(4):
-        for copy in slot_copies[plane]:
+    for side in range(2):
+        for copy in slot_copies[side]:
             copy.wait_recv()
-        grid_own[plane] = full_dot(scatter, slot_recv[plane].reshape(slots, cols))
-        copy = exchange.copy(grid_own.at[plane], grid_next.at[plane], at(behind(1), core))
+        gridded = pick_dot(
+            scatter,
+            jnp.concatenate(
+                [slot_recv[side, :, plane].reshape(slots, width) for plane in range(4)], axis=1
+            ),
+        )
+        grid_own[side] = gridded
+        copy = exchange.copy(grid_own.at[side], grid_next.at[side], at(behind(1), core))
 
         @pl.when(me > 0)
         def _():
@@ -302,13 +396,17 @@
     own_lanes = pl.ds(pl.multiple_of(core * cols, cols), cols)
     fields[2, 8 : 8 + rows, own_lanes] = (1 + mask_ref[...]).astype(jnp.float32) * 0.25
     combined = []
-    for plane in range(4):
+    for side in range(2):
 
         @pl.when(me < last)
         def _():
-            seam_copies[plane].wait_recv()
-
-        combined.append(grid_own[plane] + full_dot(seam_pick, grid_next[plane]))
+            seam_copies[side].wait_recv()
+
+        combined.append(grid_own[side] + pick_dot(seam_pick, grid_next[side]))
+    combined = [
+        jnp.concatenate([part[:, plane * width : (plane + 1) * width] for part in combined], axis=1)
+        for plane in range(4)
+    ]
     magnitude = jnp.sqrt(combined[2] * combined[3]) + EPSILON
     fields[0, 8 : 8 + rows, own_lanes] = combined[0] / magnitude
     fields[1, 8 : 8 + rows, own_lanes] = combined[1] / magnitude
@@ -426,9 +524,11 @@
 
         return finish
 
+    basis = [basis_ref[part] for part in range(3)]
+
     def precondition(turn, values, meanwhile):
-        half_basis = basis_ref[pl.ds(pl.multiple_of(core * cols, cols), cols), :]
-        spectrum = full_dot(half_basis, values, (1, 1))
+        half_basis = [basis_ref[part, own_lanes, :] for part in range(3)]
+        spectrum = basis_dot(values, half_basis, 1).T
         half = pencil // 2
         for dest in range(peers):
             base = dest * pencil
@@ -457,8 +557,8 @@
             ],
             axis=0,
         )
-        filtered = full_dot(columns, basis_ref[...], (1, 1)) / divisor
-        restored = full_dot(filtered, basis_ref[...])
+        filtered = basis_dot(columns, basis, 1) / divisor
+        restored = basis_dot(filtered, basis, 0)
         margin = jnp.zeros((pencil, rows // 2), jnp.float32)
         padded = jnp.concatenate([margin, restored, margin], axis=1)
         for dest in range(peers):
@@ -490,7 +590,7 @@
         sent.extend(copies + relays)
         window = back_recv[turn].reshape(length, 2 * rows).T
         start = rows // 2 - 8
-        return full_dot(window[start : start + rows + 16], basis_ref[...]), extra
+        return basis_dot(window[start : start + rows + 16], basis, 0), extra
 
     z0, _ = precondition(0, right_side, lambda: None)
     z0_mid = z0[8 : 8 + rows]
@@ -509,8 +609,8 @@
     alpha1 = rho1 / (energy1 + 2.0 * beta * cross + beta * beta * energy0)
     answer = alpha0 * z0_mid + alpha1 * (z1_mid + beta * z0_mid)
     left = r1 - alpha1 * (q1 + beta * w0)
-    out_ref[...] = jnp.where(core == 0, answer[:, :cols], answer[:, cols:])
-    res_ref[...] = jnp.where(core == 0, left[:, :cols], left[:, cols:])
+    out_ref[0] = jnp.where(core == 0, answer[:, :cols], answer[:, cols:])
+    out_ref[1] = jnp.where(core == 0, left[:, :cols], left[:, cols:])
 
     for copy in sent:
         copy.wait_send()
@@ -536,10 +636,11 @@
         and length <= 1024
         and peers * capacity == 128
         and cols % (16 * peers) == 0
-    )
-
-
-def unwrap_in_kernel(sums, line_target, seam_partner, mask_level, peers):
+        and cols == 256
+    )
+
+
+def unwrap_in_kernel(reference_slc, secondary_slc, line_target, seam_partner, mask_level, peers):
     rows, cols = mask_level.shape
     length = rows * peers
     capacity = max(2, 2 * rows // peers)
@@ -551,25 +652,37 @@
     )
     lam = 4.0 * np.sin(freq * (math.pi / (2.0 * length))) ** 2
     pencil = cols // peers
-    copies = 4 * (peers - 1) + (peers - 1) + 4 + 5 + 2 * (3 * (peers - 1) + 1) + 2 * (peers - 1)
+    half = reference_slc.shape[2] // 2
+    width = half // LOOK_RG
+    group = (np.arange(half)[:, None] // LOOK_RG == np.arange(width)[None, :]).astype(jnp.bfloat16)
+    parts, rest = [], basis
+    for _ in range(3):
+        parts.append(rest.astype(jnp.bfloat16))
+        rest = rest - parts[-1].astype(np.float64)
+    hbm = pl.BlockSpec(memory_space=pl.ANY)
+    copies = 2 * (peers - 1) + (peers - 1) + 2 + 5 + 2 * (3 * (peers - 1) + 1) + 2 * (peers - 1)
     vmem = pl.BlockSpec(memory_space=pltpu.VMEM)
-    shape = jax.ShapeDtypeStruct((rows, cols), jnp.float32)
 
     def scratch(*dims):
         return pltpu.VMEM(dims, jnp.float32)
 
-    return pl.pallas_call(
+    both = pl.pallas_call(
         functools.partial(unwrap_kernel, peers, capacity, damping),
-        out_shape=(shape, shape),
-        in_specs=[vmem] * 8,
-        out_specs=(vmem, vmem),
+        out_shape=jax.ShapeDtypeStruct((2, rows, cols), jnp.float32),
+        in_specs=[hbm] * 2 + [vmem] * 7,
+        out_specs=vmem,
         scratch_shapes=[
-            scratch(4, peers, capacity, cols),
-            scratch(4, peers, capacity, cols),
+            pltpu.VMEM((2, 2, rows * LOOK_AZ, half), jnp.bfloat16),
+            pltpu.VMEM((2, 2, rows * LOOK_AZ, half), jnp.bfloat16),
+            scratch(half // 128, 4 * LINES, 128),
+            scratch(2, 4, rows, width),
+            pltpu.SemaphoreType.DMA((2, rows * LOOK_AZ // LINES, 2)),
+            scratch(2, peers, 4, capacity, width),
+            scratch(2, peers, 4, capacity, width),
             scratch(peers, 8, 128),
             scratch(peers, 8, 128),
-            scratch(4, rows, cols),
-            scratch(4, rows, cols),
+            scratch(2, rows, 4 * width),
+            scratch(2, rows, 4 * width),
             scratch(3, rows + 16, length),
             scratch(2, peers, pencil // 2, 2 * rows),
             scratch(2, peers, pencil // 2, 2 * rows),
@@ -583,15 +696,29 @@
         compiler_params=pltpu.CompilerParams(collective_id=0, has_side_effects=True),
         name="unwrap",
     )(
-        sums,
+        reference_slc,
+        secondary_slc,
+        group,
         line_target.reshape(1, rows),
-        line_target.reshape(rows, 1),
-        seam_partner.reshape(rows, 1),
+        seam_partner.reshape(1, rows),
         mask_level,
-        basis.astype(np.float32),
+        np.stack(parts),
         lam.astype(np.float32)[None, :],
         lam.astype(np.float32)[:, None],
     )
+    shape = jax.ShapeDtypeStruct((rows, cols), jnp.float32)
+    return pl.pallas_call(
+        part_kernel,
+        out_shape=(shape, shape),
+        in_specs=[vmem],
+        out_specs=(vmem, vmem),
+        name="part",
+    )(both)
+
+
+def part_kernel(both_ref, first_ref, second_ref):
+    first_ref[...] = both_ref[0]
+    second_ref[...] = both_ref[1]
 
 
 def single_product(left, right):
@@ -605,9 +732,11 @@
     rg_place = lax.axis_index("rg")
     row_count = line_target.shape[0]
     col_count = mask_level.shape[1]
+    if fits_kernel(dev_count, rg_count, row_count, col_count):
+        return unwrap_in_kernel(
+            reference_slc, secondary_slc, line_target, seam_partner, mask_level, dev_count
+        )
     local_sums = form_looks(reference_slc, secondary_slc, col_count)
-    if fits_kernel(dev_count, rg_count, row_count, col_count):
-        return unwrap_in_kernel(local_sums, line_target, seam_partner, mask_level, dev_count)
     capacity = max(2, 2 * row_count // dev_count)
     owners = line_target // row_count
     local_index = jnp.arange(row_count, dtype=jnp.int32)

time: 83.5 us -> 69 us (0.83)
  Pallas kernels: 76.7 us -> 68.2 us
  local copies, waits for them, and re-layouts: 5.66 us -> 0 us
    pallas_call x1, Pallas kernels: 12.4 us -> 1.56 us  [unwrap_in_kernel(): pl.pallas_call(part_kernel, out_shape=(shape, shape), in_specs=[vmem], ou...]
    unnamed x2 -> x0, local copies, waits for them, and re-layouts: 2.95 us -> none
    reshape x2 -> x0, local copies, waits for them, and re-layouts: 2.72 us -> none  [the longest x1 1.36 us: unwrap_in_kernel(): seam_partner.reshape(rows, 1)]
    pallas_call x1, Pallas kernels: 64.3 us -> 66.6 us  [unwrap_in_kernel(): pl.pallas_call(functools.partial(unwrap_kernel, peers, capacity, damping)...]
where the time goes in v3:
time: 69 us; the launch traced here: 68.8 us
  Pallas kernels  68.2 us (99%)
    pallas_call x1, Pallas kernels, unwrap_in_kernel(): pl.pallas_call(functools.partial(unwrap_kernel, peers, capacity, damping)...  66.6 us
    pallas_call x1, Pallas kernels, unwrap_in_kernel(): pl.pallas_call(part_kernel, out_shape=(shape, shape), in_specs=[vmem], ou...  1.56 us

profile of v3, /device:TPU:0, one launch (start us, length us, event | category | flops | bytes accessed | tf_op | source)
XLA Modules:
  0.0 68.8 jit_solution(5857360729613768540)
XLA Ops:
  0.6 66.6 %unwrap.1.both_ref = f32[2,64,256]{2,1,0:T(8,128)} custom-call(bf16[2,256,5120]{2,1,0:T(8,128)(2,1)} %ref_ref.1, bf16[2,256,5120]{2,1,0:T(8,128)(2,1)} %sec_ref.1, bf16[2560,128]{1,0:T(8,128)(2,1)} %constant.8.clone.group_ref, s32[1,64]{1,0:T(1,128)} %bitcast.2, s32[1,64]{1,0:T(1,128)} %bitcast.3, s32[64,256]{1,0:T(8,128)} %mask_ref.1, ...), custom_call_target="tpu_custom_call" | custom-call | tf_op jit(solution)/shard_map/unwrap/pallas_call | solution.py:669
  67.2 1.6 %part.1 = (f32[64,256]{1,0:T(8,128)}, f32[64,256]{1,0:T(8,128)}) custom-call(f32[2,64,256]{2,1,0:T(8,128)} %unwrap.1.both_ref), custom_call_target="tpu_custom_call" | custom-call | tf_op jit(solution)/shard_map/part/pallas_call | solution.py:710

commit v4 on v3

--- a/solution.py
+++ b/solution.py
@@ -284,6 +284,15 @@
                 )
                 loads[side, index, which].start()
 
+    def facing(offset):
+        peer = me
+        bit = 1
+        while bit < peers:
+            if offset & bit:
+                peer = peer + bit - 2 * bit * (me // bit % 2)
+            bit *= 2
+        return peer
+
     barrier = pltpu.get_barrier_semaphore()
     for offset in range(peers):
         for side in (core, other):
@@ -325,9 +334,9 @@
         place_send[dest] = jnp.broadcast_to(line, (8, slots))
     pl.semaphore_wait(barrier, 2 * peers - 1)
     place_copies = []
-    for offset in range(1, peers):
+    for offset in range(peers - 1, 0, -1):
         copy = exchange.copy(
-            place_send.at[ahead(offset)], place_recv.at[me], at(ahead(offset), core)
+            place_send.at[facing(offset)], place_recv.at[me], at(facing(offset), core)
         )
         copy.start()
         place_copies.append(copy)
@@ -346,11 +355,11 @@
                 peers, capacity, width
             )
         side_copies = []
-        for offset in range(1, peers):
+        for offset in range(peers - 1, 0, -1):
             copy = exchange.copy(
-                slot_send.at[side, ahead(offset)],
+                slot_send.at[side, facing(offset)],
                 slot_recv.at[side, me],
-                at(ahead(offset), core),
+                at(facing(offset), core),
             )
             copy.start()
             side_copies.append(copy)
@@ -506,9 +515,9 @@
         dot_send[turn] = tile
         dot_recv[turn, me] = tile
         copies = []
-        for offset in range(1, peers):
+        for offset in range(peers - 1, 0, -1):
             copy = exchange.copy(
-                dot_send.at[turn], dot_recv.at[turn, me], at(ahead(offset), core)
+                dot_send.at[turn], dot_recv.at[turn, me], at(facing(offset), core)
             )
             copy.start()
             copies.append(copy)
@@ -536,11 +545,11 @@
                 [spectrum[base : base + half], spectrum[base + half : base + pencil]], axis=1
             )
         copies = []
-        for offset in range(1, peers):
+        for offset in range(peers - 1, 0, -1):
             copy = exchange.copy(
-                spec_send.at[turn, ahead(offset)],
+                spec_send.at[turn, facing(offset)],
                 spec_recv.at[turn, me],
-                at(ahead(offset), core),
+                at(facing(offset), core),
             )
             copy.start()
             copies.append(copy)
@@ -564,11 +573,11 @@
         for dest in range(peers):
             back_send[turn, dest] = padded[:, dest * rows : (dest + 2) * rows]
         copies = []
-        for offset in range(1, peers):
+        for offset in range(peers - 1, 0, -1):
             copy = exchange.copy(
-                back_send.at[turn, ahead(offset)],
+                back_send.at[turn, facing(offset)],
                 back_recv.at[turn, core, me],
-                at(ahead(offset), core),
+                at(facing(offset), core),
             )
             copy.start()
             copies.append(copy)
@@ -580,8 +589,8 @@
         ]
         relays[0].start()
         for offset in range(1, peers):
-            copies[offset - 1].wait_recv()
-            held = back_recv.at[turn, core, behind(offset)]
+            copies[peers - 1 - offset].wait_recv()
+            held = back_recv.at[turn, core, facing(offset)]
             relay = exchange.copy(held, held, at(me, other))
             relay.start()
             relays.append(relay)
@@ -637,6 +646,7 @@
         and peers * capacity == 128
         and cols % (16 * peers) == 0
         and cols == 256
+        and peers & (peers - 1) == 0
     )
 
 

time: 69 us -> 67.6 us (0.980)
  Pallas kernels: 68.2 us -> 66.8 us
    pallas_call x1, Pallas kernels: 66.6 us -> 65.2 us  [unwrap_in_kernel(): pl.pallas_call(functools.partial(unwrap_kernel, peers, capacity, damping)...]
where the time goes in v4:
time: 67.6 us; the launch traced here: 67.4 us
  Pallas kernels  66.8 us (99%)
    pallas_call x1, Pallas kernels, unwrap_in_kernel(): pl.pallas_call(functools.partial(unwrap_kernel, peers, capacity, damping)...  65.2 us
    pallas_call x1, Pallas kernels, unwrap_in_kernel(): pl.pallas_call(part_kernel, out_shape=(shape, shape), in_specs=[vmem], ou...  1.56 us

profile of v4, /device:TPU:0, one launch (start us, length us, event | category | flops | bytes accessed | tf_op | source)
XLA Modules:
  0.0 67.4 jit_solution(15218854298329844308)
XLA Ops:
  0.6 65.2 %unwrap.1.both_ref = f32[2,64,256]{2,1,0:T(8,128)} custom-call(bf16[2,256,5120]{2,1,0:T(8,128)(2,1)} %ref_ref.1, bf16[2,256,5120]{2,1,0:T(8,128)(2,1)} %sec_ref.1, bf16[2560,128]{1,0:T(8,128)(2,1)} %constant.8.clone.group_ref, s32[1,64]{1,0:T(1,128)} %bitcast.2, s32[1,64]{1,0:T(1,128)} %bitcast.3, s32[64,256]{1,0:T(8,128)} %mask_ref.1, ...), custom_call_target="tpu_custom_call" | custom-call | tf_op jit(solution)/shard_map/unwrap/pallas_call | solution.py:679
  65.9 1.6 %part.1 = (f32[64,256]{1,0:T(8,128)}, f32[64,256]{1,0:T(8,128)}) custom-call(f32[2,64,256]{2,1,0:T(8,128)} %unwrap.1.both_ref), custom_call_target="tpu_custom_call" | custom-call | tf_op jit(solution)/shard_map/part/pallas_call | solution.py:720
